TPU v7x, 32 devices: a whole 2x2x4 slice. The times are simulated.
32 devices in a mesh: rep: 4 (over y, x), dp: 8 (over z, core).
Axes of the slice: x: 2, y: 2, z: 4, core: 2. Of those that a mesh axis runs over, the one named last changes fastest.
Arguments:
- pixels: int32 [64, 144, 196], P(('rep', 'dp')), may hold values from 0 to 255
- return_ids: int32 [64, 4], P(('rep', 'dp')), may hold values from 0 to 119
- action_ids: int32 [64, 4], P(('rep', 'dp')), may hold values from 0 to 17
- reward_ids: int32 [64, 4], P(('rep', 'dp')), may hold values from 0 to 3
- type_map: int32 [64, 156], P(('rep', 'dp')), may hold values from 0 to 3, as said below
- expert_flags: int32 [64], P(('rep', 'dp')), may hold values 0 or 1
- inner_step: int32 [1], replicated, may hold values from 2 to 20
- attention_weight: float32 [4, 1792, 1792], P(None, 'dp')
- attention_drift: float32 [4, 4, 1792, 1792], P('rep', None, 'dp'), may hold values from -0.02734375 to 0.02734375
- attention_moment: float32 [4, 4, 1792, 1792], P('rep', None, 'dp'), may hold values from -0.00010681152 to 0.00010681152
- attention_square: float32 [4, 4, 1792, 1792], P('rep', None, 'dp'), may hold values from 1.3354959e-09 to 5.2915876e-09
- attention_velocity: float32 [4, 1792, 1792], P(None, 'dp'), may hold values from -0.0625 to 0.0625
- feedforward_weight: float32 [2, 1792, 7168], P(None, 'dp'), may hold values from -0.125 to 0.125
- feedforward_drift: float32 [4, 2, 1792, 7168], P('rep', None, 'dp'), may hold values from -0.02734375 to 0.02734375
- feedforward_moment: float32 [4, 2, 1792, 7168], P('rep', None, 'dp'), may hold values from -0.00010681152 to 0.00010681152
- feedforward_square: float32 [4, 2, 1792, 7168], P('rep', None, 'dp'), may hold values from 1.3354959e-09 to 5.2915876e-09
- feedforward_velocity: float32 [2, 1792, 7168], P(None, 'dp'), may hold values from -0.0625 to 0.0625
- embedding_weight: float32 [494, 1792], P(None, 'dp')
- embedding_drift: float32 [4, 494, 1792], P('rep', None, 'dp'), may hold values from -0.625 to 0.625
- embedding_moment: float32 [4, 494, 1792], P('rep', None, 'dp'), may hold values from -0.00010681152 to 0.00010681152
- embedding_square: float32 [4, 494, 1792], P('rep', None, 'dp'), may hold values from 1.3354959e-09 to 5.2915876e-09
- embedding_velocity: float32 [494, 1792], P(None, 'dp'), may hold values from -0.625 to 0.625
- readout_weight: float32 [142, 1792], P(None, 'dp'), may hold values from -0.25 to 0.25
- readout_drift: float32 [4, 142, 1792], P('rep', None, 'dp'), may hold values from -0.0546875 to 0.0546875
- readout_moment: float32 [4, 142, 1792], P('rep', None, 'dp'), may hold values from -0.0004272461 to 0.0004272461
- readout_square: float32 [4, 142, 1792], P('rep', None, 'dp'), may hold values from 2.141833e-08 to 8.567332e-08
- readout_velocity: float32 [142, 1792], P(None, 'dp'), may hold values from -0.125 to 0.125
- gains_weight: float32 [6, 1792], P(None, 'dp')
- gains_drift: float32 [4, 6, 1792], P('rep', None, 'dp'), may hold values from -0.625 to 0.625
- gains_moment: float32 [4, 6, 1792], P('rep', None, 'dp'), may hold values from -0.0008544922 to 0.0008544922
- gains_square: float32 [4, 6, 1792], P('rep', None, 'dp'), may hold values from 8.567332e-08 to 3.401735e-07
- gains_velocity: float32 [6, 1792], P(None, 'dp'), may hold values from -0.625 to 0.625
Outputs:
- loss: float32 [4], P('rep')
- gradient_norm: float32 [4], P('rep')
- updated_attention: float32 [4, 1792, 1792], P(None, 'dp')
- moment_attention: float32 [4, 4, 1792, 1792], P('rep', None, 'dp')
- square_attention: float32 [4, 4, 1792, 1792], P('rep', None, 'dp')
- velocity_attention: float32 [4, 1792, 1792], P(None, 'dp')
- updated_feedforward: float32 [2, 1792, 7168], P(None, 'dp')
- moment_feedforward: float32 [4, 2, 1792, 7168], P('rep', None, 'dp')
- square_feedforward: float32 [4, 2, 1792, 7168], P('rep', None, 'dp')
- velocity_feedforward: float32 [2, 1792, 7168], P(None, 'dp')
- updated_embedding: float32 [494, 1792], P(None, 'dp')
- moment_embedding: float32 [4, 494, 1792], P('rep', None, 'dp')
- square_embedding: float32 [4, 494, 1792], P('rep', None, 'dp')
- velocity_embedding: float32 [494, 1792], P(None, 'dp')
- updated_readout: float32 [142, 1792], P(None, 'dp')
- moment_readout: float32 [4, 142, 1792], P('rep', None, 'dp')
- square_readout: float32 [4, 142, 1792], P('rep', None, 'dp')
- velocity_readout: float32 [142, 1792], P(None, 'dp')
- updated_gains: float32 [6, 1792], P(None, 'dp')
- moment_gains: float32 [4, 6, 1792], P('rep', None, 'dp')
- square_gains: float32 [4, 6, 1792], P('rep', None, 'dp')
- velocity_gains: float32 [6, 1792], P(None, 'dp')
Inputs may be any that keep to these rules, and one draw needn't show every extreme that they name: `type_map`: in each sequence the timesteps that carry marks are its last ones, one or more; such a timestep holds 1, 2, 3 at its positions 35, 36, 37; every other position holds 0.
All inputs are finite; a program needn't handle non-finite values. No bound on the sum of `expert_flags` on one device may be relied on, other than what follows from the above.
Results may differ from a plain program's by a relative error of at most 0.02.
Values may be sent and summed in bfloat16 or wider, within the bound.
No kernel may reach another device: no remote copies, remote signals or barrier semaphores. Data moves between devices by JAX's collectives and lax.ppermute only.
A program may use at most 704 MiB of HBM per device.

v0:
```python
import jax
import jax.numpy as jnp
from jax import lax
from jax.sharding import PartitionSpec as P

D = 1792
HEADS = 14
HEAD_DIM = 128
PATCH_PIXELS = 196
RETURN_BINS = 120
ACTION_BINS = 18
PATCHES = 36
TIMESTEPS = 4
SPAN = 39
LENGTH = 156
HEAD_ROWS = 142


EPS_NORM = 1e-05
BETA_ONE = 0.9
BETA_TWO = 0.95
ADAM_EPS = 1e-08
CLIP = 1.0
OUTER_MOMENTUM = 0.9
OUTER_RATE = 0.7
RATES = (0.05, 0.05, 0.3, 0.1, 0.4)
DECAYS = (0.1, 0.1, 0.0, 0.1, 0.0)
NEGATIVE = -1e30
HIGHEST = lax.Precision.HIGHEST


def as_sent(value):
    return jax.tree.map(lambda a: a.astype(jnp.bfloat16) if a.dtype == jnp.float32 else a, value)


def layer_norm(values, gain, shift):
    centered = values - jnp.mean(values, axis=-1, keepdims=True)
    variance = jnp.mean(centered * centered, axis=-1, keepdims=True)
    return centered * lax.rsqrt(variance + EPS_NORM) * gain + shift


def gelu(values):
    return (
        0.5
        * values
        * (1.0 + jnp.tanh(0.7978845608028654 * (values + 0.044715 * values * values * values)))
    )


def norm_backward(values, gain, shift, upstream):
    unused, pull = jax.vjp(layer_norm, values, gain, shift)
    return pull(upstream)


def attention_scores(queries, key_rows):
    causal = jnp.arange(LENGTH)[:, None] >= jnp.arange(LENGTH)[None, :]
    raw = jnp.einsum("bqhe,bkhe->bhqk", queries, key_rows, preferred_element_type=jnp.float32) * (
        1.0 / HEAD_DIM**0.5
    )
    return jnp.where(causal, raw, NEGATIVE)


def head_terms(rows, targets, weights, readout, denoms):
    logits = jnp.einsum("nd,vd->nv", rows, readout, preferred_element_type=jnp.float32)
    columns = jnp.arange(HEAD_ROWS, dtype=jnp.int32)
    kinds = (targets >= RETURN_BINS).astype(jnp.int32) + (
        targets >= RETURN_BINS + ACTION_BINS
    ).astype(jnp.int32)
    lower = jnp.where(kinds == 0, 0, jnp.where(kinds == 1, RETURN_BINS, RETURN_BINS + ACTION_BINS))
    upper = jnp.where(
        kinds == 0, RETURN_BINS, jnp.where(kinds == 1, RETURN_BINS + ACTION_BINS, HEAD_ROWS)
    )
    allowed = (columns[None, :] >= lower[:, None]) & (columns[None, :] < upper[:, None])
    masked = jnp.where(allowed, logits, NEGATIVE)
    highest_logit = jnp.max(masked, axis=-1, keepdims=True)
    expos = jnp.exp(masked - highest_logit)
    totals = jnp.sum(expos, axis=-1, keepdims=True)
    onehot = (columns[None, :] == targets[:, None]).astype(jnp.float32)
    chosen = jnp.sum(onehot * logits, axis=-1)
    cross = highest_logit[:, 0] + jnp.log(totals[:, 0]) - chosen
    kind_hits = (kinds[:, None] == jnp.arange(3, dtype=jnp.int32)[None, :]).astype(jnp.float32)
    sums = jnp.sum((weights * cross)[:, None] * kind_hits, axis=0)
    scale = weights / jnp.sum(kind_hits * denoms[None, :], axis=-1)
    slope = (scale[:, None] * (expos / totals - onehot)).astype(jnp.bfloat16)
    readout_grad = jnp.einsum("nv,nd->vd", slope, rows, preferred_element_type=jnp.float32)
    row_grad = jnp.einsum("nv,vd->nd", slope, readout, preferred_element_type=jnp.float32).astype(
        jnp.bfloat16
    )
    return (sums, readout_grad, row_grad)


def shards(
    pixels,
    return_ids,
    action_ids,
    reward_ids,
    type_map,
    expert_flags,
    inner_step,
    attention_weight,
    attention_drift,
    attention_moment,
    attention_square,
    attention_velocity,
    feedforward_weight,
    feedforward_drift,
    feedforward_moment,
    feedforward_square,
    feedforward_velocity,
    embedding_weight,
    embedding_drift,
    embedding_moment,
    embedding_square,
    embedding_velocity,
    readout_weight,
    readout_drift,
    readout_moment,
    readout_square,
    readout_velocity,
    gains_weight,
    gains_drift,
    gains_moment,
    gains_square,
    gains_velocity,
):
    shared = (attention_weight, feedforward_weight, embedding_weight, readout_weight, gains_weight)
    drifts = (attention_drift, feedforward_drift, embedding_drift, readout_drift, gains_drift)
    moments = (attention_moment, feedforward_moment, embedding_moment, readout_moment, gains_moment)
    squares_old = (
        attention_square,
        feedforward_square,
        embedding_square,
        readout_square,
        gains_square,
    )
    velocities = (
        attention_velocity,
        feedforward_velocity,
        embedding_velocity,
        readout_velocity,
        gains_velocity,
    )
    local = tuple((weight + drift[0] for weight, drift in zip(shared, drifts)))
    rounded = tuple((weight.astype(jnp.bfloat16) for weight in local))
    attention_full, feedforward_full, embedding_full, readout_full, gains_full = jax.tree.map(
        lambda part, own: part.astype(own.dtype),
        lax.all_gather(as_sent(rounded), "dp", axis=1, tiled=True),
        rounded,
    )
    gains = gains_full.astype(jnp.float32)
    count = pixels.shape[0]
    rows_total = count * LENGTH
    pixel_rows = (
        (pixels.astype(jnp.float32) / 127.5 - 1.0)
        .astype(jnp.bfloat16)
        .reshape(count * TIMESTEPS * PATCHES, PATCH_PIXELS)
    )
    patches = jnp.dot(pixel_rows, embedding_full[:PATCH_PIXELS], preferred_element_type=jnp.float32)
    targets = jnp.stack(
        [return_ids, action_ids + RETURN_BINS, reward_ids + RETURN_BINS + ACTION_BINS], axis=-1
    )
    columns = jnp.arange(HEAD_ROWS, dtype=jnp.int32)
    token_hits = (targets[..., None] == columns).astype(jnp.bfloat16)
    tokens = jnp.einsum(
        "btjv,vd->btjd",
        token_hits,
        embedding_full[PATCH_PIXELS : PATCH_PIXELS + HEAD_ROWS],
        preferred_element_type=jnp.float32,
    )
    position = embedding_full[PATCH_PIXELS + HEAD_ROWS :].astype(jnp.float32)
    stream = (
        jnp.concatenate([patches.reshape(count, TIMESTEPS, PATCHES, D), tokens], axis=2).reshape(
            count, LENGTH, D
        )
        + position
    )
    normed = layer_norm(stream, gains[0], gains[1]).astype(jnp.bfloat16)
    triple = jnp.einsum(
        "bld,hde->hble", normed, attention_full[:3], preferred_element_type=jnp.float32
    ).astype(jnp.bfloat16)
    queries = triple[0].reshape(count, LENGTH, HEADS, HEAD_DIM)
    key_rows = triple[1].reshape(count, LENGTH, HEADS, HEAD_DIM)
    value_rows = triple[2].reshape(count, LENGTH, HEADS, HEAD_DIM)
    scores = attention_scores(queries, key_rows)
    highest_score = jnp.max(scores, axis=-1, keepdims=True)
    log_total = highest_score + jnp.log(
        jnp.sum(jnp.exp(scores - highest_score), axis=-1, keepdims=True)
    )
    probs = jnp.exp(scores - log_total)
    mixed = jnp.einsum(
        "bhqk,bkhe->bqhe",
        probs.astype(jnp.bfloat16),
        value_rows,
        preferred_element_type=jnp.float32,
    )
    mixed = mixed.astype(jnp.bfloat16).reshape(count, LENGTH, D)
    stream_one = stream + jnp.einsum(
        "bld,de->ble", mixed, attention_full[3], preferred_element_type=jnp.float32
    )
    normed_two = layer_norm(stream_one, gains[2], gains[3]).astype(jnp.bfloat16)
    hidden = jnp.einsum(
        "bld,df->blf", normed_two, feedforward_full[0], preferred_element_type=jnp.float32
    )
    activated = gelu(hidden).astype(jnp.bfloat16)
    stream_two = stream_one + jnp.einsum(
        "blf,df->bld", activated, feedforward_full[1], preferred_element_type=jnp.float32
    )
    final = layer_norm(stream_two, gains[4], gains[5]).astype(jnp.bfloat16)
    marks = (
        type_map.reshape(count, TIMESTEPS, SPAN)[:, :, PATCHES - 1 : PATCHES + 2]
        == jnp.arange(1, 4, dtype=jnp.int32)
    ).astype(jnp.float32)
    boost = jnp.array([2.0, 0.0, 0.0], dtype=jnp.float32)
    weights = marks * (1.0 + boost * expert_flags.astype(jnp.float32)[:, None, None])
    denoms = lax.psum(jnp.sum(weights, axis=(0, 1)), "dp")
    devices = lax.axis_size("dp")
    here = lax.axis_index("dp")
    per_device = TIMESTEPS * count
    capacity = 4 * per_device // devices
    peer = jnp.arange(devices, dtype=jnp.int32)[:, None]
    slot = jnp.arange(capacity, dtype=jnp.int32)[None, :]
    member = peer % 4
    kinds = jnp.maximum(member - 1, 0)
    owners = jnp.where(kinds == 0, devices // 2, devices // 4)
    owner_rank = jnp.where(kinds == 0, 2 * (peer // 4) + member, peer // 4)
    item = (owner_rank - here * per_device) % owners + slot * owners
    valid = item < per_device
    item = jnp.where(valid, item, 0)
    sequence = item // TIMESTEPS
    moment_index = item % TIMESTEPS
    flat_item = ((sequence * TIMESTEPS + moment_index) * 3 + kinds).reshape(-1)
    place = (sequence * LENGTH + moment_index * SPAN + PATCHES - 1 + kinds).reshape(-1)
    send_rows = jnp.take(final.reshape(rows_total, D), place, axis=0).reshape(devices, capacity, D)
    send_target = jnp.take(targets.reshape(-1), flat_item).reshape(devices, capacity)
    send_weight = jnp.where(
        valid, jnp.take(weights.reshape(-1), flat_item).reshape(devices, capacity), 0.0
    )
    labels = jnp.stack([send_target.astype(jnp.float32), send_weight], axis=-1).astype(jnp.bfloat16)
    got_rows, got_labels = (
        lax.all_to_all(send_rows, "dp", split_axis=0, concat_axis=0, tiled=True),
        lax.all_to_all(labels, "dp", split_axis=0, concat_axis=0, tiled=True),
    )
    got_labels = got_labels.astype(jnp.float32).reshape(-1, 2)
    sums, readout_grad, row_grad = head_terms(
        got_rows.reshape(-1, D),
        got_labels[:, 0].astype(jnp.int32),
        got_labels[:, 1],
        readout_full,
        denoms,
    )
    returned = lax.all_to_all(
        row_grad.reshape(devices, capacity, D), "dp", split_axis=0, concat_axis=0, tiled=True
    )
    returned = jnp.where(valid[..., None], returned.astype(jnp.float32), 0.0).reshape(-1, D)
    final_grad = jnp.zeros((rows_total, D), jnp.float32).at[place].add(returned)
    totals = lax.psum(sums, "dp")
    grad_two, gain_five, shift_five = norm_backward(
        stream_two, gains[4], gains[5], final_grad.reshape(count, LENGTH, D)
    )
    output_grad = grad_two.astype(jnp.bfloat16)
    activated_grad = jnp.einsum(
        "bld,df->blf", output_grad, feedforward_full[1], preferred_element_type=jnp.float32
    )
    unused, gelu_pull = jax.vjp(gelu, hidden)
    hidden_grad = gelu_pull(activated_grad)[0].astype(jnp.bfloat16)
    normed_two_grad = jnp.einsum(
        "blf,df->bld", hidden_grad, feedforward_full[0], preferred_element_type=jnp.float32
    )
    width = D // lax.axis_size("dp")
    offset = lax.axis_index("dp") * width
    normed_piece = lax.all_gather(normed_two, "dp", axis=0, tiled=True)
    output_piece = lax.all_gather(output_grad, "dp", axis=0, tiled=True)
    hidden_piece = lax.all_gather(hidden_grad, "dp", axis=0, tiled=True)
    activated_piece = lax.all_gather(activated, "dp", axis=0, tiled=True)
    normed_cols = lax.dynamic_slice_in_dim(normed_piece, offset, width, 2)
    output_cols = lax.dynamic_slice_in_dim(output_piece, offset, width, 2)
    up_part = jnp.einsum(
        "bld,blf->df", normed_cols, hidden_piece, preferred_element_type=jnp.float32
    )
    down_part = jnp.einsum(
        "bld,blf->df", output_cols, activated_piece, preferred_element_type=jnp.float32
    )
    feedforward_grad = jnp.stack([up_part, down_part])
    part_one, gain_three, shift_three = norm_backward(
        stream_one, gains[2], gains[3], normed_two_grad
    )
    grad_one = grad_two + part_one
    branch_grad = grad_one.astype(jnp.bfloat16)
    output_proj_grad = jnp.einsum(
        "bld,ble->de", mixed, branch_grad, preferred_element_type=jnp.float32
    )
    mixed_grad = jnp.einsum(
        "ble,de->bld", branch_grad, attention_full[3], preferred_element_type=jnp.float32
    )
    mixed_grad = mixed_grad.astype(jnp.bfloat16).reshape(count, LENGTH, HEADS, HEAD_DIM)
    probs = jnp.exp(attention_scores(queries, key_rows) - log_total)
    value_grad = jnp.einsum(
        "bhqk,bqhe->bkhe",
        probs.astype(jnp.bfloat16),
        mixed_grad,
        preferred_element_type=jnp.float32,
    )
    prob_grad = jnp.einsum(
        "bqhe,bkhe->bhqk", mixed_grad, value_rows, preferred_element_type=jnp.float32
    )
    score_grad = (probs * (prob_grad - jnp.sum(probs * prob_grad, axis=-1, keepdims=True))).astype(
        jnp.bfloat16
    )
    query_grad = jnp.einsum(
        "bhqk,bkhe->bqhe", score_grad, key_rows, preferred_element_type=jnp.float32
    ) * (1.0 / HEAD_DIM**0.5)
    key_grad = jnp.einsum(
        "bhqk,bqhe->bkhe", score_grad, queries, preferred_element_type=jnp.float32
    ) * (1.0 / HEAD_DIM**0.5)
    triple_grad = (
        jnp.stack([query_grad, key_grad, value_grad])
        .astype(jnp.bfloat16)
        .reshape(3, count, LENGTH, D)
    )
    projection_grads = jnp.einsum(
        "bld,hble->hde", normed, triple_grad, preferred_element_type=jnp.float32
    )
    normed_grad = jnp.einsum(
        "hble,hde->bld", triple_grad, attention_full[:3], preferred_element_type=jnp.float32
    )
    part_zero, gain_one, shift_one = norm_backward(stream, gains[0], gains[1], normed_grad)
    grad_zero = grad_one + part_zero
    zero_grid = grad_zero.reshape(count, TIMESTEPS, SPAN, D)
    patch_grad = (
        zero_grid[:, :, :PATCHES].astype(jnp.bfloat16).reshape(count * TIMESTEPS * PATCHES, D)
    )
    pixel_grad = jnp.einsum("np,nd->pd", pixel_rows, patch_grad, preferred_element_type=jnp.float32)
    table_grad = jnp.einsum(
        "btjv,btjd->vd",
        token_hits.astype(jnp.float32),
        zero_grid[:, :, PATCHES:],
        precision=HIGHEST,
        preferred_element_type=jnp.float32,
    )
    position_grad = jnp.sum(grad_zero, axis=0)
    embedding_grad = jnp.concatenate([pixel_grad, table_grad, position_grad], axis=0)
    attention_grad = jnp.concatenate([projection_grads, output_proj_grad[None]], axis=0)
    gains_grad = jnp.stack([gain_one, shift_one, gain_three, shift_three, gain_five, shift_five])
    attention_grad, embedding_grad, readout_grad, gains_grad = (
        lax.psum_scatter(attention_grad, "dp", scatter_dimension=1, tiled=True),
        lax.psum_scatter(embedding_grad, "dp", scatter_dimension=1, tiled=True),
        lax.psum_scatter(readout_grad, "dp", scatter_dimension=1, tiled=True),
        lax.psum_scatter(gains_grad, "dp", scatter_dimension=1, tiled=True),
    )
    grads = (attention_grad, feedforward_grad, embedding_grad, readout_grad, gains_grad)
    local_squares = sum((jnp.sum(grad * grad) for grad in grads))
    total_squares = lax.psum(local_squares, "dp")
    gradient_norm = jnp.sqrt(total_squares)
    loss = jnp.sum(totals / denoms)
    factor = CLIP / jnp.maximum(gradient_norm, CLIP)
    steps = inner_step[0].astype(jnp.float32)
    bias_one = 1.0 - jnp.power(jnp.float32(BETA_ONE), steps)
    bias_two = 1.0 - jnp.power(jnp.float32(BETA_TWO), steps)
    new_locals, new_moments, new_squares = ([], [], [])
    for group_index in range(5):
        clipped = grads[group_index] * factor
        moment = BETA_ONE * moments[group_index][0] + (1.0 - BETA_ONE) * clipped
        square = BETA_TWO * squares_old[group_index][0] + (1.0 - BETA_TWO) * clipped * clipped
        update = (
            moment / bias_one / (jnp.sqrt(square / bias_two) + ADAM_EPS)
            + DECAYS[group_index] * local[group_index]
        )
        new_locals.append(local[group_index] - RATES[group_index] * update)
        new_moments.append(moment)
        new_squares.append(square)
    summed = lax.psum(tuple(new_locals), "rep")
    replicas = lax.axis_size("rep")
    outputs = [loss[None], gradient_norm[None]]
    for group_index in range(5):
        delta = shared[group_index] - summed[group_index] / replicas
        velocity = OUTER_MOMENTUM * velocities[group_index] + delta
        updated = shared[group_index] - OUTER_RATE * (delta + OUTER_MOMENTUM * velocity)
        outputs.append(updated)
        outputs.append(new_moments[group_index][None])
        outputs.append(new_squares[group_index][None])
        outputs.append(velocity)
    return tuple(outputs)


def solution(mesh):
    placed = (
        P(("rep", "dp"), None, None),
        P(("rep", "dp"), None),
        P(("rep", "dp"), None),
        P(("rep", "dp"), None),
        P(("rep", "dp"), None),
        P(("rep", "dp")),
        P(),
        P(None, "dp", None),
        P("rep", None, "dp", None),
        P("rep", None, "dp", None),
        P("rep", None, "dp", None),
        P(None, "dp", None),
        P(None, "dp", None),
        P("rep", None, "dp", None),
        P("rep", None, "dp", None),
        P("rep", None, "dp", None),
        P(None, "dp", None),
        P(None, "dp"),
        P("rep", None, "dp"),
        P("rep", None, "dp"),
        P("rep", None, "dp"),
        P(None, "dp"),
        P(None, "dp"),
        P("rep", None, "dp"),
        P("rep", None, "dp"),
        P("rep", None, "dp"),
        P(None, "dp"),
        P(None, "dp"),
        P("rep", None, "dp"),
        P("rep", None, "dp"),
        P("rep", None, "dp"),
        P(None, "dp"),
    )
    return jax.shard_map(
        shards,
        mesh=mesh,
        in_specs=placed,
        out_specs=(
            P("rep"),
            P("rep"),
            P(None, "dp", None),
            P("rep", None, "dp", None),
            P("rep", None, "dp", None),
            P(None, "dp", None),
            P(None, "dp", None),
            P("rep", None, "dp", None),
            P("rep", None, "dp", None),
            P(None, "dp", None),
            P(None, "dp"),
            P("rep", None, "dp"),
            P("rep", None, "dp"),
            P(None, "dp"),
            P(None, "dp"),
            P("rep", None, "dp"),
            P("rep", None, "dp"),
            P(None, "dp"),
            P(None, "dp"),
            P("rep", None, "dp"),
            P("rep", None, "dp"),
            P(None, "dp"),
        ),
        check_vma=False,
    )
```

profile of v0, /device:TPU:0, one launch (start us, length us, event | category | flops | bytes accessed | tf_op | source)
XLA Modules:
  0.0 2783.0 jit_solution(8503410451871057370)
XLA Ops:
  16.3 12.1 fusion.22
  38.7 14.6 all-gather
  53.6 27.1 all-gather.1
  81.4 17.8 psum.57
  117.3 153.5 %all-gather.12.cloned.1.call-done = bf16[4,1792,1792]{2,1,0:T(8,128)(2,1)} async-done(((bf16[4,224,1792]{2,1,0:T(8,128)(2,1)}), bf16[4,1792,1792]{2,1,0:T(8,128)(2,1)}) %all-gather.12.cloned.1.call-update) | async-done | bytes 25690128 | tf_op jit(solution)/shard_map/all_gather | solution.py:147
  270.8 10.9 fusion.25
  311.6 394.6 %all-gather.14.cloned.1.call-done = bf16[2,1792,7168]{2,1,0:T(8,128)(2,1)} async-done(((bf16[2,224,7168]{2,1,0:T(8,128)(2,1)}), bf16[2,1792,7168]{2,1,0:T(8,128)(2,1)}) %all-gather.14.cloned.1.call-update) | async-done | bytes 51380240 | tf_op jit(solution)/shard_map/all_gather | solution.py:147
  706.2 17.1 multiply_convert_fusion
  723.4 16.9 fusion.126
  762.1 8.9 all_to_all.15
  783.4 21.9 fusion.16
  805.4 22.2 multiply_reduce_fusion.4
  869.4 12.6 fusion.117
  920.9 19.7 convolution_bitcast_fusion
  940.6 33.5 %pad_maximum_fusion = f32[4,1792,1792]{2,1,0:T(8,128)} fusion(f32[1,1792,1792]{2,1,0:T(8,128)} %convolution_bitcast_fusion.1, f32[3,1792,1792]{2,1,0:T(8,128)} %convolution_bitcast_fusion), kind=kLoop, calls=%fused_computation.4 | loop fusion | flops 12845056 | bytes 102760448 | tf_op jit(solution)/shard_map/concatenate | solution.py:342
  978.3 27.4 reduce-scatter.13.cloned.1.call-done
  1007.6 86.8 %all-gather.20.cloned.1.call-done = bf16[16,156,1792]{2,1,0:T(8,128)(2,1)} async-done(((bf16[2,156,1792]{2,1,0:T(8,128)(2,1)}), bf16[16,156,1792]{2,1,0:T(8,128)(2,1)}) %all-gather.20.cloned.1.call-update) | async-done | bytes 8945680 | tf_op jit(solution)/shard_map/all_gather | solution.py:272
  1094.3 316.8 %all-gather.22.cloned.1.call-done = bf16[16,156,7168]{2,1,0:T(8,128)(2,1)} async-done(((bf16[2,156,7168]{2,1,0:T(8,128)(2,1)}), bf16[16,156,7168]{2,1,0:T(8,128)(2,1)}) %all-gather.22.cloned.1.call-update) | async-done | bytes 35782672 | tf_op jit(solution)/shard_map/all_gather | solution.py:274
  1411.1 21.0 fusion.37
  1432.2 68.2 %all-gather.16.cloned.1.call-done = bf16[16,156,1792]{2,1,0:T(8,128)(2,1)} async-done(((bf16[2,156,1792]{2,1,0:T(8,128)(2,1)}), bf16[16,156,1792]{2,1,0:T(8,128)(2,1)}) %all-gather.16.cloned.1.call-update) | async-done | bytes 8945680 | tf_op jit(solution)/shard_map/all_gather | solution.py:271
  1500.4 316.6 %all-gather.18.cloned.1.call-done = bf16[16,156,7168]{2,1,0:T(8,128)(2,1)} async-done(((bf16[2,156,7168]{2,1,0:T(8,128)(2,1)}), bf16[16,156,7168]{2,1,0:T(8,128)(2,1)}) %all-gather.18.cloned.1.call-update) | async-done | bytes 35782672 | tf_op jit(solution)/shard_map/all_gather | solution.py:273
  1817.0 20.5 fusion.39
  1837.5 8.7 multiply_reduce_fusion
  1846.2 465.2 %reduce-scatter.11.cloned.1.call-done = f32[4,224,1792]{2,1,0:T(8,128)} async-done(((f32[4,1792,1792]{2,1,0:T(8,128)}), f32[4,224,1792]{2,1,0:T(8,128)}) %reduce-scatter.11.cloned.1.call-update) | async-done | bytes 6422544 | tf_op jit(solution)/shard_map/reduce_scatter | solution.py:345
  2319.8 14.4 all-reduce
  2335.7 27.5 multiply_subtract_fusion.2
  2364.7 17.6 fusion.41
  2385.8 10.6 psum.63
  2397.7 23.9 fusion.12
  2421.5 320.3 %all-reduce.4.cloned.1.call-done = (f32[4,224,1792]{2,1,0:T(8,128)}, f32[2,224,7168]{2,1,0:T(8,128)}, f32[494,224]{0,1:T(8,128)}, f32[142,224]{1,0:T(8,128)}) async-done(((f32[4,224,1792]{2,1,0:T(8,128)}, f32[2,224,7168]{2,1,0:T(8,128)}, f32[494,224]{0,1:T(8,128)}, f32[142,224]{1,0:T(8,128)}), (f32[4,224,1792]{2,1,0:T(8,128)}, f32[2,224,7168]{2,1,0:T(8,128)}, f32[494,224]{0,1:T(8,128)}, ...) | async-done | bytes 19837456 | tf_op jit(solution)/shard_map/psum | solution.py:371
  2741.8 22.1 multiply_subtract_fusion
  2764.3 8.6 multiply_subtract_fusion.3
  (411 shorter events, 201.7 us)
Async XLA Ops:
  7.2 95.3 %all-gather.10.cloned.1.call-start = ((), (), s32[]{:S(2)}) async-start(), calls=%async_computation.7 | async-start | bytes 2064384 | tf_op jit(solution)/shard_map/all_gather | solution.py:147
  9.2 261.6 %all-gather.12.cloned.1.call-start = ((), (), s32[]{:S(2)}) async-start(), calls=%async_computation.8 | async-start | bytes 28901376 | tf_op jit(solution)/shard_map/all_gather | solution.py:147
  16.2 690.0 %all-gather.14.cloned.1.call-start = ((), (), s32[]{:S(2)}) async-start(), calls=%async_computation.9 | async-start | bytes 57802752 | tf_op jit(solution)/shard_map/all_gather | solution.py:147
  32.1 69.0 %all-to-all-start = ((bf16[8,4,2]{1,2,0:T(2,128)(2,1)}), bf16[8,4,2]{1,2,0:T(2,128)(2,1)S(1)}, u32[]{:S(2)}, u32[]{:S(2)}) async-start(bf16[8,4,2]{1,2,0:T(2,128)(2,1)} %copy.206), calls=%async_computation | async-start | bytes 8192 | tf_op jit(solution)/shard_map/all_to_all | solution.py:241
  38.6 62.5 %copy-start.82 = (s32[2,4,3]{1,2,0:T(4,128)}, s32[2,4,3]{1,2,0:T(4,128)S(1)}, u32[]{:S(2)}) copy-start(s32[2,4,3]{1,2,0:T(4,128)S(1)} %copy.212) | copy-start | bytes 292
  53.4 243.8 %copy-start.32 = (pred[156,156]{0,1:T(8,128)(4,1)}, pred[156,156]{0,1:T(8,128)(4,1)S(1)}, u32[]{:S(2)}) copy-start(pred[156,156]{0,1:T(8,128)(4,1)S(1)} %iota_compare_fusion) | copy-start | bytes 73012
  53.5 256.6 %copy-start.52 = (f32[1792]{0:T(1024)}, f32[1792]{0:T(1024)S(1)}, u32[]{:S(2)}) copy-start(f32[1792]{0:T(1024)S(1)} %get-tuple-element.144) | copy-start | bytes 21508
  53.5 687.2 %copy-start.50 = (f32[1792]{0:T(1024)}, f32[1792]{0:T(1024)S(1)}, u32[]{:S(2)}) copy-start(f32[1792]{0:T(1024)S(1)} %get-tuple-element.141) | copy-start | bytes 21508
  101.9 646.9 %copy-start.101 = (s32[32,1]{0,1:T(1,128)}, s32[32,1]{0,1:T(1,128)S(1)}, u32[]{:S(2)}) copy-start(s32[32,1]{0,1:T(1,128)S(1)} %get-tuple-element.174) | copy-start | bytes 388
  104.5 199.6 %copy-start.9 = (f32[156,1792]{1,0:T(8,128)}, f32[156,1792]{1,0:T(8,128)S(1)}, u32[]{:S(2)}) copy-start(f32[156,1792]{1,0:T(8,128)S(1)} %convert_element_type.135) | copy-start | bytes 3354628
  112.3 191.8 %copy-start.1 = (f32[2,156,1792]{2,1,0:T(8,128)}, f32[2,156,1792]{2,1,0:T(8,128)S(1)}, u32[]{:S(2)}) copy-start(f32[2,156,1792]{2,1,0:T(8,128)S(1)} %reshape.1002) | copy-start | bytes 6709252
  115.7 166.1 %copy-start.78 = (f32[2,156]{1,0:T(2,128)}, f32[2,156]{1,0:T(2,128)S(1)}, u32[]{:S(2)}) copy-start(f32[2,156]{1,0:T(2,128)S(1)} %add.744) | copy-start | bytes 3748
  115.7 166.1 %copy-start.64 = (f32[2,156]{1,0:T(2,128)}, f32[2,156]{1,0:T(2,128)S(1)}, u32[]{:S(2)}) copy-start(f32[2,156]{1,0:T(2,128)S(1)} %rsqrt.33) | copy-start | bytes 3748
  309.7 413.6 %copy-start.68 = (f32[2,156]{1,0:T(2,128)}, f32[2,156]{1,0:T(2,128)S(1)}, u32[]{:S(2)}) copy-start(f32[2,156]{1,0:T(2,128)S(1)} %broadcast_multiply_fusion.2) | copy-start | bytes 3748
  310.1 413.2 %copy-start.74 = (f32[2,156]{1,0:T(2,128)}, f32[2,156]{1,0:T(2,128)S(1)}, u32[]{:S(2)}) copy-start(f32[2,156]{1,0:T(2,128)S(1)} %multiply_reduce_fusion.10) | copy-start | bytes 3748
  310.2 413.2 %copy-start.80 = (f32[2,156]{1,0:T(2,128)}, f32[2,156]{1,0:T(2,128)S(1)}, u32[]{:S(2)}) copy-start(f32[2,156]{1,0:T(2,128)S(1)} %fusion.100) | copy-start | bytes 3748
  311.6 411.8 %copy-start.21 = (bf16[2,156,1792]{2,1,0:T(8,128)(2,1)}, bf16[2,156,1792]{2,1,0:T(8,128)(2,1)S(1)}, u32[]{:S(2)}) copy-start(bf16[2,156,1792]{2,1,0:T(8,128)(2,1)S(1)} %add_convert_fusion.1) | copy-start | bytes 3354628
  745.4 9.9 all-to-all-start.1
  748.7 226.3 %reduce-scatter.17.cloned.1.call-start = ((), (), s32[]{:S(2)}) async-start(), calls=%async_computation.17 | async-start | bytes 1032192
  892.2 84.3 %reduce-scatter.15.cloned.1.call-start = ((), (), s32[]{:S(2)}) async-start(), calls=%async_computation.16 | async-start | bytes 2064384
  894.8 110.8 %reduce-scatter.13.cloned.1.call-start = ((), (), s32[]{:S(2)}) async-start(), calls=%async_computation.15 | async-start | bytes 4128768
  910.9 183.4 %all-gather.20.cloned.1.call-start = ((), (), s32[]{:S(2)}) async-start(), calls=%async_computation.13 | async-start | bytes 10321920 | tf_op jit(solution)/shard_map/all_gather | solution.py:272
  911.7 499.5 %all-gather.22.cloned.1.call-start = ((), (), s32[]{:S(2)}) async-start(), calls=%async_computation.14 | async-start | bytes 41287680 | tf_op jit(solution)/shard_map/all_gather | solution.py:274
  912.4 588.0 %all-gather.16.cloned.1.call-start = ((), (), s32[]{:S(2)}) async-start(), calls=%async_computation.11 | async-start | bytes 10321920 | tf_op jit(solution)/shard_map/all_gather | solution.py:271
  913.2 903.9 %all-gather.18.cloned.1.call-start = ((), (), s32[]{:S(2)}) async-start(), calls=%async_computation.12 | async-start | bytes 41287680 | tf_op jit(solution)/shard_map/all_gather | solution.py:273
  913.8 1397.7 %reduce-scatter.11.cloned.1.call-start = ((), (), s32[]{:S(2)}) async-start(), calls=%async_computation.10 | async-start | bytes 57802752 | tf_op jit(solution)/shard_map/reduce_scatter | solution.py:345
  974.2 1767.6 %all-reduce.4.cloned.1.call-start = ((), (), s32[]{:S(2)}) async-start(), calls=%async_computation.18 | async-start | bytes 39747584 | tf_op jit(solution)/shard_map/psum | solution.py:371
  1846.2 473.6 %copy-start.100 = (f32[3]{0:T(128)S(1)}, f32[3]{0:T(128)}, u32[]{:S(2)}) copy-start(f32[3]{0:T(128)} %get-tuple-element.150) | copy-start | bytes 40
  1846.2 488.7 %copy-start.28 = (f32[142,224]{1,0:T(8,128)S(1)}, f32[142,224]{1,0:T(8,128)}, u32[]{:S(2)}) copy-start(f32[142,224]{1,0:T(8,128)} %param.55) | copy-start | bytes 381700
  1846.2 488.7 %copy-start.35 = (f32[1,142,224]{2,0,1:T(1,128)S(1)}, f32[1,142,224]{2,0,1:T(1,128)}, u32[]{:S(2)}) copy-start(f32[1,142,224]{2,0,1:T(1,128)} %param.56) | copy-start | bytes 381700
  1846.2 488.7 %copy-start.46 = (f32[1,142,224]{2,0,1:T(1,128)S(1)}, f32[1,142,224]{2,0,1:T(1,128)}, u32[]{:S(2)}) copy-start(f32[1,142,224]{2,0,1:T(1,128)} %param.58) | copy-start | bytes 381700
  1846.2 488.7 %copy-start.47 = (f32[1,142,224]{2,0,1:T(1,128)S(1)}, f32[1,142,224]{2,0,1:T(1,128)}, u32[]{:S(2)}) copy-start(f32[1,142,224]{2,0,1:T(1,128)} %param.57) | copy-start | bytes 381700
  (89 other events, 943.5 us)
Sparse Core Ops, SparseCore 0:
  10.2 29.6 all-gather.9
  42.1 228.6 all-gather.11
  273.0 433.2 all-gather.13
  892.4 30.8 reduce-scatter.16
  926.1 33.3 reduce-scatter.14
  962.3 43.2 reduce-scatter.12
  1007.4 86.9 all-gather.19
  1096.7 314.4 all-gather.21
  1412.9 87.4 all-gather.15
  1502.5 314.4 all-gather.17
  1819.5 491.8 reduce-scatter.10
  2382.5 359.2 all-reduce.3
where the time goes:
time: 2790 us; the launch traced here: 2780 us
  waiting for transfers between devices  2160 us (77%)
  other arithmetic  214 us (8%)
  matrix products  210 us (8%)
  blocking collectives  93.3 us (3%)
  local copies, waits for them, and re-layouts  75.4 us (3%)
    all_gather x3, waiting for transfers between devices, shards(): lax.all_gather(as_sent(rounded), 'dp', axis=1, tiled=True)  548 us
    reduce_scatter x1, waiting for transfers between devices, shards(): lax.psum_scatter(attention_grad, 'dp', scatter_dimension=1, tiled=True)  465 us
    psum x1, waiting for transfers between devices, shards(): summed = lax.psum(tuple(new_locals), 'rep')  320 us
    all_gather x1, waiting for transfers between devices, shards(): activated_piece = lax.all_gather(activated, 'dp', axis=0, tiled=True)  317 us
    all_gather x1, waiting for transfers between devices, shards(): hidden_piece = lax.all_gather(hidden_grad, 'dp', axis=0, tiled=True)  317 us
    all_gather x1, waiting for transfers between devices, shards(): output_piece = lax.all_gather(output_grad, 'dp', axis=0, tiled=True)  86.8 us
    all_gather x1, waiting for transfers between devices, shards(): normed_piece = lax.all_gather(normed_two, 'dp', axis=0, tiled=True)  68.2 us
  transfers between devices with their start and end apart: 14, of which 10 were waited for; matrix products, arithmetic and copies ran while one was open for 9% of the time, Pallas kernels for 0%

commit v1 on v0

v1 whole, which is shorter than its diff:
```python
import jax
import jax.numpy as jnp
from jax import lax
from jax.sharding import PartitionSpec as P

D = 1792
FF = 7168
HEADS = 14
HEAD_DIM = 128
PATCH_PIXELS = 196
RETURN_BINS = 120
ACTION_BINS = 18
PATCHES = 36
TIMESTEPS = 4
SPAN = 39
LENGTH = 156
HEAD_ROWS = 142
PICKS = 3 * TIMESTEPS

EPS_NORM = 1e-05
BETA_ONE = 0.9
BETA_TWO = 0.95
ADAM_EPS = 1e-08
CLIP = 1.0
OUTER_MOMENTUM = 0.9
OUTER_RATE = 0.7
RATES = (0.05, 0.05, 0.3, 0.1, 0.4)
DECAYS = (0.1, 0.1, 0.0, 0.1, 0.0)
NEGATIVE = -1e30
SCALE = 1.0 / HEAD_DIM**0.5
F32 = jnp.float32
BF16 = jnp.bfloat16


def dot(spec, left, right):
    return jnp.einsum(spec, left, right, preferred_element_type=F32)


def gelu(values):
    return (
        0.5
        * values
        * (1.0 + jnp.tanh(0.7978845608028654 * (values + 0.044715 * values * values * values)))
    )


def gather_rows(piece):
    return lax.all_gather(piece, "dp", axis=0, tiled=True)


def gather_columns(piece):
    whole = lax.all_gather(piece, "dp", axis=0)
    return jnp.moveaxis(whole, 0, 1).reshape(piece.shape[0], -1)


def scatter_rows(partial):
    count = lax.axis_size("dp")
    parts = partial.astype(BF16).reshape((count, partial.shape[0] // count) + partial.shape[1:])
    mine = lax.all_to_all(parts, "dp", split_axis=0, concat_axis=0, tiled=True)
    return jnp.sum(mine.astype(F32), axis=0)


def scatter_columns(partial):
    count = lax.axis_size("dp")
    parts = partial.astype(BF16).reshape(partial.shape[0], count, partial.shape[1] // count)
    mine = lax.all_to_all(
        jnp.moveaxis(parts, 1, 0), "dp", split_axis=0, concat_axis=0, tiled=True
    )
    return jnp.sum(mine.astype(F32), axis=0)


def sum_rows(partial):
    return gather_rows(scatter_rows(partial).astype(BF16))


def norm_rows(values):
    centered = values - jnp.mean(values, axis=-1, keepdims=True)
    inverse = lax.rsqrt(jnp.mean(centered * centered, axis=-1, keepdims=True) + EPS_NORM)
    return centered * inverse, inverse


def norm_rows_back(scaled, inverse, gain, upstream):
    shaped = upstream * gain
    first = jnp.mean(shaped, axis=-1, keepdims=True)
    second = jnp.mean(shaped * scaled, axis=-1, keepdims=True)
    return inverse * (shaped - first - scaled * second)


def own_columns(values, width):
    return lax.dynamic_slice_in_dim(
        values, lax.axis_index("dp") * width, width, values.ndim - 1
    )


def swap_hidden(weight):
    count = lax.axis_size("dp")
    here = lax.axis_index("dp")
    piece = FF // count
    width = weight.shape[1]
    result = jnp.zeros((2, D, piece), weight.dtype)
    for step in range(count):
        peer = here ^ step
        block = lax.dynamic_slice_in_dim(weight, peer * piece, piece, 2)
        if step:
            block = lax.ppermute(block, "dp", [(i, i ^ step) for i in range(count)])
        result = lax.dynamic_update_slice_in_dim(result, block, peer * width, 1)
    return result


def shards(
    pixels,
    return_ids,
    action_ids,
    reward_ids,
    type_map,
    expert_flags,
    inner_step,
    attention_weight,
    attention_drift,
    attention_moment,
    attention_square,
    attention_velocity,
    feedforward_weight,
    feedforward_drift,
    feedforward_moment,
    feedforward_square,
    feedforward_velocity,
    embedding_weight,
    embedding_drift,
    embedding_moment,
    embedding_square,
    embedding_velocity,
    readout_weight,
    readout_drift,
    readout_moment,
    readout_square,
    readout_velocity,
    gains_weight,
    gains_drift,
    gains_moment,
    gains_square,
    gains_velocity,
):
    shared = (attention_weight, feedforward_weight, embedding_weight, readout_weight, gains_weight)
    drifts = (attention_drift, feedforward_drift, embedding_drift, readout_drift, gains_drift)
    moments = (attention_moment, feedforward_moment, embedding_moment, readout_moment, gains_moment)
    squares_old = (
        attention_square,
        feedforward_square,
        embedding_square,
        readout_square,
        gains_square,
    )
    velocities = (
        attention_velocity,
        feedforward_velocity,
        embedding_velocity,
        readout_velocity,
        gains_velocity,
    )
    attention_low, feedforward_low, embedding_low, readout_low, gains_low = (
        (weight + drift[0]).astype(BF16) for weight, drift in zip(shared, drifts)
    )
    count = pixels.shape[0]
    devices = lax.axis_size("dp")
    seqs = count * devices
    width = D // devices
    rows = seqs * PICKS
    here = lax.axis_index("dp")

    pixel_rows = (pixels.astype(F32) / 127.5 - 1.0).astype(BF16)
    targets = jnp.stack(
        [return_ids, action_ids + RETURN_BINS, reward_ids + RETURN_BINS + ACTION_BINS], axis=-1
    )
    marks = (
        type_map.reshape(count, TIMESTEPS, SPAN)[:, :, PATCHES - 1 : PATCHES + 2]
        == jnp.arange(1, 4, dtype=jnp.int32)
    ).astype(F32)
    boost = jnp.array([2.0, 0.0, 0.0], dtype=F32)
    weights = marks * (1.0 + boost * expert_flags.astype(F32)[:, None, None])
    labels = jnp.stack([targets.astype(BF16), weights.astype(BF16)], axis=-1)
    labels = jnp.pad(labels, ((0, 0), (0, 0), (0, 0), (0, PATCH_PIXELS - 2)))
    packed = jnp.concatenate(
        [pixel_rows.reshape(count, TIMESTEPS, PATCHES, PATCH_PIXELS), labels], axis=2
    ).reshape(count, LENGTH, PATCH_PIXELS)
    packed = gather_rows(packed)
    small_full = lax.all_gather(jnp.concatenate([readout_low, gains_low], axis=0), "dp", axis=0)
    small_full = jnp.moveaxis(small_full, 0, 1).reshape(HEAD_ROWS + 6, D)
    readout_full = small_full[:HEAD_ROWS]
    gains_full = small_full[HEAD_ROWS:].astype(F32)
    gains_own = gains_low.astype(F32)
    hidden_weights = swap_hidden(feedforward_low)

    labels = packed.reshape(seqs, TIMESTEPS, SPAN, PATCH_PIXELS)[:, :, PATCHES:, :2].astype(F32)
    targets = labels[..., 0].astype(jnp.int32).reshape(rows)
    weights = labels[..., 1].reshape(rows)
    token_target = jnp.where(
        jnp.arange(LENGTH) % SPAN >= PATCHES, packed[:, :, 0].astype(F32), -1.0
    )
    is_token = (jnp.arange(LENGTH) % SPAN >= PATCHES)[None, :, None]
    features = jnp.concatenate(
        [
            jnp.where(is_token, 0.0, packed.astype(F32)).astype(BF16),
            (token_target[..., None] == jnp.arange(HEAD_ROWS, dtype=F32)).astype(BF16),
            jnp.broadcast_to(jnp.eye(LENGTH, dtype=BF16), (seqs, LENGTH, LENGTH)),
        ],
        axis=-1,
    ).reshape(seqs * LENGTH, -1)
    stream = dot("tv,vd->td", features, embedding_low)

    own_mean = jnp.mean(stream, axis=-1)
    own_square = jnp.sum(jnp.square(stream - own_mean[:, None]), axis=-1)
    stats = lax.all_gather(jnp.stack([own_mean, own_square]), "dp", axis=0)
    mean = jnp.mean(stats[:, 0], axis=0)
    variance = (
        jnp.sum(stats[:, 1], axis=0) + width * jnp.sum(jnp.square(stats[:, 0] - mean), axis=0)
    ) / D
    inverse = lax.rsqrt(variance + EPS_NORM)[:, None]
    scaled = (stream - mean[:, None]) * inverse
    normed = (scaled * gains_own[0] + gains_own[1]).astype(BF16).reshape(seqs, LENGTH, width)

    def picked(values):
        grid = values.reshape(seqs, TIMESTEPS, SPAN, width)
        return grid[:, :, PATCHES - 1 : PATCHES + 2].reshape(rows, width)

    query_weight, key_weight, value_weight, output_weight = attention_low
    key_weight = key_weight.reshape(width, HEADS, HEAD_DIM)
    value_weight = value_weight.reshape(width, HEADS, HEAD_DIM)
    normed_picked = picked(normed)
    queries = sum_rows(dot("rd,de->re", normed_picked, query_weight))
    queries = queries.reshape(rows, HEADS, HEAD_DIM)

    def by_sequence(values):
        grid = values.reshape(HEADS, seqs, PICKS, values.shape[-1])
        return jnp.swapaxes(grid, 0, 1).reshape(seqs, HEADS * PICKS, -1)

    def by_head(values):
        grid = values.reshape(seqs, HEADS, PICKS, values.shape[-1])
        return jnp.swapaxes(grid, 0, 1).reshape(HEADS, rows, -1)

    reach = by_sequence(dot("rhe,dhe->hrd", queries, key_weight).astype(BF16))
    scores = scatter_rows(dot("sqd,skd->sqk", reach, normed)) * SCALE
    place = (
        SPAN * (jnp.arange(PICKS) // 3) + PATCHES - 1 + jnp.arange(PICKS) % 3
    )
    seen = jnp.tile(jnp.arange(LENGTH)[None, :] <= place[:, None], (HEADS, 1))
    scores = jnp.where(seen, scores, NEGATIVE)
    expos = jnp.exp(scores - jnp.max(scores, axis=-1, keepdims=True))
    probs = expos / jnp.sum(expos, axis=-1, keepdims=True)
    probs_all = gather_rows(probs.astype(BF16))
    blend = by_head(dot("sqk,skd->sqd", probs_all, normed).astype(BF16))
    mixed_part = dot("hrd,dhe->rhe", blend, value_weight).reshape(rows, D)
    mixed = scatter_columns(mixed_part).astype(BF16)
    branch = scatter_columns(dot("rd,de->re", mixed, output_weight))
    stream_one = gather_columns((picked(stream) + branch).astype(BF16)).astype(F32)

    scaled_one, inverse_one = norm_rows(stream_one)
    normed_two = (scaled_one * gains_full[2] + gains_full[3]).astype(BF16)
    hidden = dot("rd,df->rf", normed_two, hidden_weights[0])
    activated = gelu(hidden).astype(BF16)
    stream_two = stream_one + sum_rows(
        dot("rf,df->rd", activated, hidden_weights[1])
    ).astype(F32)
    scaled_two, inverse_two = norm_rows(stream_two)
    final = (scaled_two * gains_full[4] + gains_full[5]).astype(BF16)

    kinds = jnp.arange(rows) % 3
    kind_hits = (kinds[:, None] == jnp.arange(3)[None, :]).astype(F32)
    denoms = jnp.sum(weights[:, None] * kind_hits, axis=0)
    columns = jnp.arange(HEAD_ROWS, dtype=jnp.int32)
    lower = jnp.where(kinds == 0, 0, jnp.where(kinds == 1, RETURN_BINS, RETURN_BINS + ACTION_BINS))
    upper = jnp.where(
        kinds == 0, RETURN_BINS, jnp.where(kinds == 1, RETURN_BINS + ACTION_BINS, HEAD_ROWS)
    )
    allowed = (columns[None, :] >= lower[:, None]) & (columns[None, :] < upper[:, None])
    logits = dot("rd,vd->rv", final, readout_full)
    masked = jnp.where(allowed, logits, NEGATIVE)
    highest = jnp.max(masked, axis=-1, keepdims=True)
    expos = jnp.exp(masked - highest)
    totals = jnp.sum(expos, axis=-1, keepdims=True)
    onehot = (columns[None, :] == targets[:, None]).astype(F32)
    cross = highest[:, 0] + jnp.log(totals[:, 0]) - jnp.sum(onehot * logits, axis=-1)
    loss = jnp.sum(jnp.sum((weights * cross)[:, None] * kind_hits, axis=0) / denoms)
    scale = weights / jnp.sum(kind_hits * denoms, axis=-1)
    slope = (scale[:, None] * (expos / totals - onehot)).astype(BF16)
    readout_grad = dot("rv,rd->vd", slope, own_columns(final, width))
    final_grad = dot("rv,vd->rd", slope, readout_full).astype(BF16).astype(F32)

    shift_five = own_columns(jnp.sum(final_grad, axis=0), width)
    gain_five = own_columns(jnp.sum(final_grad * scaled_two, axis=0), width)
    grad_two = norm_rows_back(scaled_two, inverse_two, gains_full[4], final_grad)
    output_grad = grad_two.astype(BF16)
    activated_grad = dot("rd,df->rf", output_grad, hidden_weights[1])
    unused, gelu_pull = jax.vjp(gelu, hidden)
    hidden_grad = gelu_pull(activated_grad)[0].astype(BF16)
    normed_two_grad = sum_rows(dot("rf,df->rd", hidden_grad, hidden_weights[0])).astype(F32)
    unit_rows = lax.all_gather(jnp.stack([hidden_grad, activated]), "dp", axis=0)
    unit_rows = jnp.transpose(unit_rows, (1, 2, 0, 3)).reshape(2, rows, FF)
    feedforward_grad = jnp.stack(
        [
            dot("rd,rf->df", own_columns(normed_two, width), unit_rows[0]),
            dot("rd,rf->df", own_columns(output_grad, width), unit_rows[1]),
        ]
    )
    shift_three = own_columns(jnp.sum(normed_two_grad, axis=0), width)
    gain_three = own_columns(jnp.sum(normed_two_grad * scaled_one, axis=0), width)
    grad_one = grad_two + norm_rows_back(scaled_one, inverse_one, gains_full[2], normed_two_grad)
    branch_grad = grad_one.astype(BF16)

    output_proj_grad = dot("rd,re->de", mixed, branch_grad)
    mixed_grad = gather_columns(dot("re,de->rd", branch_grad, output_weight).astype(BF16))
    mixed_grad = mixed_grad.reshape(rows, HEADS, HEAD_DIM)
    blend_grad_heads = dot("rhe,dhe->hrd", mixed_grad, value_weight).astype(BF16)
    value_weight_grad = dot("hrd,rhe->dhe", blend, mixed_grad).reshape(width, D)
    blend_grad = by_sequence(blend_grad_heads)
    prob_grad = scatter_rows(dot("sqd,skd->sqk", blend_grad, normed))
    score_grad = probs * (prob_grad - jnp.sum(probs * prob_grad, axis=-1, keepdims=True))
    score_grad = gather_rows((score_grad * SCALE).astype(BF16))
    reach_grad = by_head(dot("sqk,skd->sqd", score_grad, normed).astype(BF16))
    query_grad = sum_rows(dot("hrd,dhe->rhe", reach_grad, key_weight).reshape(rows, D))
    key_weight_grad = dot("hrd,rhe->dhe", reach_grad, queries).reshape(width, D)
    query_weight_grad = dot("rd,re->de", normed_picked, query_grad)
    normed_grad = dot("sqk,sqd->skd", probs_all, blend_grad) + dot(
        "sqk,sqd->skd", score_grad, reach
    )
    through_query = dot("re,de->rd", query_grad, query_weight)

    def spread(values):
        grid = values.reshape(seqs, TIMESTEPS, 3, width)
        return jnp.pad(
            grid, ((0, 0), (0, 0), (PATCHES - 1, SPAN - PATCHES - 2), (0, 0))
        ).reshape(seqs * LENGTH, width)

    normed_grad = normed_grad.reshape(seqs * LENGTH, width) + spread(through_query)
    shift_one = jnp.sum(normed_grad, axis=0)
    gain_one = jnp.sum(normed_grad * scaled, axis=0)
    shaped = normed_grad * gains_own[0]
    sums = jnp.stack([jnp.sum(shaped, axis=-1), jnp.sum(shaped * scaled, axis=-1)])
    sums = jnp.sum(lax.all_gather(sums, "dp", axis=0), axis=0)[..., None] / D
    grad_zero = spread(own_columns(grad_one, width)) + inverse * (
        shaped - sums[0] - scaled * sums[1]
    )
    embedding_grad = dot("tv,td->vd", features, grad_zero.astype(BF16))
    attention_grad = jnp.stack(
        [query_weight_grad, key_weight_grad, value_weight_grad, output_proj_grad]
    )
    gains_grad = jnp.stack([gain_one, shift_one, gain_three, shift_three, gain_five, shift_five])

    grads = (attention_grad, feedforward_grad, embedding_grad, readout_grad, gains_grad)
    total_squares = lax.psum(sum((jnp.sum(grad * grad) for grad in grads)), "dp")
    gradient_norm = jnp.sqrt(total_squares)
    factor = CLIP / jnp.maximum(gradient_norm, CLIP)
    steps = inner_step[0].astype(F32)
    bias_one = 1.0 - jnp.power(F32(BETA_ONE), steps)
    bias_two = 1.0 - jnp.power(F32(BETA_TWO), steps)
    changes, new_moments, new_squares = ([], [], [])
    for group in range(5):
        clipped = grads[group] * factor
        moment = BETA_ONE * moments[group][0] + (1.0 - BETA_ONE) * clipped
        square = BETA_TWO * squares_old[group][0] + (1.0 - BETA_TWO) * clipped * clipped
        drift = drifts[group][0]
        update = moment / bias_one / (jnp.sqrt(square / bias_two) + ADAM_EPS) + DECAYS[group] * (
            shared[group] + drift
        )
        changes.append((RATES[group] * update - drift).astype(BF16))
        new_moments.append(moment)
        new_squares.append(square)
    summed = lax.psum(tuple(changes), "rep")
    replicas = lax.axis_size("rep")
    outputs = [loss[None], gradient_norm[None]]
    for group in range(5):
        delta = summed[group].astype(F32) / replicas
        velocity = OUTER_MOMENTUM * velocities[group] + delta
        updated = shared[group] - OUTER_RATE * (delta + OUTER_MOMENTUM * velocity)
        outputs.append(updated)
        outputs.append(new_moments[group][None])
        outputs.append(new_squares[group][None])
        outputs.append(velocity)
    return tuple(outputs)


def solution(mesh):
    placed = (
        P(("rep", "dp"), None, None),
        P(("rep", "dp"), None),
        P(("rep", "dp"), None),
        P(("rep", "dp"), None),
        P(("rep", "dp"), None),
        P(("rep", "dp")),
        P(),
        P(None, "dp", None),
        P("rep", None, "dp", None),
        P("rep", None, "dp", None),
        P("rep", None, "dp", None),
        P(None, "dp", None),
        P(None, "dp", None),
        P("rep", None, "dp", None),
        P("rep", None, "dp", None),
        P("rep", None, "dp", None),
        P(None, "dp", None),
        P(None, "dp"),
        P("rep", None, "dp"),
        P("rep", None, "dp"),
        P("rep", None, "dp"),
        P(None, "dp"),
        P(None, "dp"),
        P("rep", None, "dp"),
        P("rep", None, "dp"),
        P("rep", None, "dp"),
        P(None, "dp"),
        P(None, "dp"),
        P("rep", None, "dp"),
        P("rep", None, "dp"),
        P("rep", None, "dp"),
        P(None, "dp"),
    )
    return jax.shard_map(
        shards,
        mesh=mesh,
        in_specs=placed,
        out_specs=(
            P("rep"),
            P("rep"),
            P(None, "dp", None),
            P("rep", None, "dp", None),
            P("rep", None, "dp", None),
            P(None, "dp", None),
            P(None, "dp", None),
            P("rep", None, "dp", None),
            P("rep", None, "dp", None),
            P(None, "dp", None),
            P(None, "dp"),
            P("rep", None, "dp"),
            P("rep", None, "dp"),
            P(None, "dp"),
            P(None, "dp"),
            P("rep", None, "dp"),
            P("rep", None, "dp"),
            P(None, "dp"),
            P(None, "dp"),
            P("rep", None, "dp"),
            P("rep", None, "dp"),
            P(None, "dp"),
        ),
        check_vma=False,
    )
```

time: 2790 us -> 1060 us (0.38)
  waiting for transfers between devices: 2160 us -> 259 us
  blocking collectives: 93.3 us -> 319 us
  matrix products: 210 us -> 53.9 us
  local copies, waits for them, and re-layouts: 75.4 us -> 177 us
  other arithmetic: 214 us -> 172 us
  starting transfers between devices: 10.4 us -> 42.2 us
    all_gather x7 -> x1, waiting for transfers between devices: 1340 us -> 0.01 us  [shards(): lax.all_gather(jnp.stack([hidden_grad, activated]), 'dp', axis=0)]
    reduce_scatter x1 -> x0, waiting for transfers between devices: 465 us -> none  [shards(): lax.psum_scatter(attention_grad, 'dp', scatter_dimension=1, tiled=True)]
    all_gather x2 -> x12, blocking collectives: 41.7 us -> 302 us  [the longest x7 123 us: gather_rows(): return lax.all_gather(piece, 'dp', axis=0, tiled=True)]
    psum x1 -> x2, waiting for transfers between devices: 320 us -> 158 us  [shards(): summed = lax.psum(tuple(changes), 'rep')]
    dot_general x24 -> x28, matrix products: 207 us -> 49.6 us  [dot(): return jnp.einsum(spec, left, right, preferred_element_type=F32)]
    all_to_all x2 -> x8, waiting for transfers between devices: 6.41 us -> 76.6 us  [the longest x6 74.7 us: scatter_rows(): mine = lax.all_to_all(parts, 'dp', split_axis=0, concat_axis=0, tiled=True)]
    convert_element_type x13 -> x23, other arithmetic: 25.6 us -> 66 us  [the longest x3 38.4 us: shards(): changes.append((RATES[group] * update - drift).astype(BF16))]
    concatenate x2, other arithmetic: 33.8 us -> 3.29 us  [the longest x1 3.06 us: shards(): jnp.concatenate([jnp.where(is_token, 0.0, packed.astype(F32)).astype(BF16...]
  transfers between devices with their start and end apart: 14 -> 18, of which waited for: 10 -> 9; matrix products, arithmetic and copies ran while one was open for 9% -> 25% of each run, Pallas kernels for 0% -> 0%
where the time goes in v1:
time: 1060 us; the launch traced here: 1050 us
  blocking collectives  319 us (30%)
  waiting for transfers between devices  259 us (24%)
  local copies, waits for them, and re-layouts  177 us (17%)
  other arithmetic  172 us (16%)
  matrix products  53.9 us (5%)
  starting transfers between devices  42.2 us (4%)
  between operations  21.6 us (2%)
    psum x2, waiting for transfers between devices, shards(): summed = lax.psum(tuple(changes), 'rep')  158 us
    all_gather x7, blocking collectives, gather_rows(): return lax.all_gather(piece, 'dp', axis=0, tiled=True)  123 us
    all_gather x1, blocking collectives, shards(): lax.all_gather(jnp.concatenate([readout_low, gains_low], axis=0), 'dp', a...  81.3 us
    all_to_all x6, waiting for transfers between devices, scatter_rows(): mine = lax.all_to_all(parts, 'dp', split_axis=0, concat_axis=0, tiled=True)  74.7 us
    all_gather x2, blocking collectives, gather_columns(): whole = lax.all_gather(piece, 'dp', axis=0)  69.5 us
    dot_general x28, matrix products, dot(): return jnp.einsum(spec, left, right, preferred_element_type=F32)  49.6 us
    convert_element_type x3, other arithmetic, shards(): changes.append((RATES[group] * update - drift).astype(BF16))  38.4 us
    sub x5, other arithmetic, shards(): updated = shared[group] - OUTER_RATE * (delta + OUTER_MOMENTUM * velocity)  31.4 us
  transfers between devices with their start and end apart: 18, of which 9 were waited for; matrix products, arithmetic and copies ran while one was open for 25% of the time, Pallas kernels for 0%

profile of v1, /device:TPU:0, one launch (start us, length us, event | category | flops | bytes accessed | tf_op | source)
XLA Modules:
  0.0 1045.1 jit_solution(10641129968883526052)
XLA Ops:
  12.8 20.6 %all_gather.55 = bf16[16,156,196]{2,1,0:T(8,128)(2,1)S(1)} all-gather(bf16[2,156,196]{2,1,0:T(8,128)(2,1)S(1)} %copy.479), channel_id=1, replica_groups=mesh['rep'=4,'dp'=8] {'dp'}, dimensions={0}, use_global_device_ids=true | all-gather | bytes 1100736 | tf_op jit(solution)/shard_map/all_gather | solution.py:48
  38.0 4.5 reshape.821
  45.6 14.0 %all-gather.5 = f32[8,2,2496]{2,1,0:T(2,128)S(1)} all-gather(f32[1,2,2496]{2,1,0:T(2,128)S(1)} %maximum_bitcast_fusion.1), channel_id=2, replica_groups=mesh['rep'=4,'dp'=8] {'dp'}, dimensions={0}, use_global_device_ids=true | all-gather | bytes 179712 | tf_op jit(solution)/shard_map/all_gather | solution.py:213
  65.9 5.3 fusion.21
  85.0 12.2 %all-to-all-done = bf16[8,24,1792]{2,1,0:T(8,128)(2,1)} async-done(((bf16[8,24,1792]{2,1,0:T(8,128)(2,1)}), bf16[8,24,1792]{2,1,0:T(8,128)(2,1)}, u32[]{:S(2)}, u32[]{:S(2)}) %all-to-all-start) | async-done | bytes 688160 | tf_op jit(solution)/shard_map/all_to_all | solution.py:59
  98.4 15.7 %all_gather.58 = bf16[192,1792]{1,0:T(8,128)(2,1)S(1)} all-gather(bf16[24,1792]{1,0:T(8,128)(2,1)S(1)} %reduce_sum.409), channel_id=1, replica_groups=mesh['rep'=4,'dp'=8] {'dp'}, dimensions={0}, use_global_device_ids=true | all-gather | bytes 774144 | tf_op jit(solution)/shard_map/all_gather | solution.py:48
  127.1 29.4 %all-to-all-done.1 = bf16[8,2,168,156]{2,1,3,0:T(2,128)(2,1)} async-done(((bf16[8,2,168,156]{2,1,3,0:T(2,128)(2,1)}), bf16[8,2,168,156]{2,1,3,0:T(2,128)(2,1)}, u32[]{:S(2)}, u32[]{:S(2)}) %all-to-all-start.1) | async-done | bytes 838688 | tf_op jit(solution)/shard_map/all_to_all | solution.py:59
  161.3 18.2 %all_gather.59 = bf16[16,168,156]{1,2,0:T(8,128)(2,1)S(1)} all-gather(bf16[2,168,156]{1,2,0:T(8,128)(2,1)S(1)} %copy.428), channel_id=1, replica_groups=mesh['rep'=4,'dp'=8] {'dp'}, dimensions={0}, use_global_device_ids=true | all-gather | bytes 943488 | tf_op jit(solution)/shard_map/all_gather | solution.py:48
  191.5 11.9 %fusion.16 = bf16[2,224,7168]{2,1,0:T(8,128)(2,1)} fusion(f32[2,224,7168]{2,1,0:T(8,128)} %param.45, f32[1,2,224,7168]{3,2,1,0:T(8,128)} %param.46), kind=kLoop, calls=%fused_computation.40 | loop fusion | flops 6422528 | bytes 32112640 | tf_op jit(solution)/shard_map/convert_element_type | solution.py:162
  216.3 81.3 %all-gather.6 = bf16[8,148,224]{2,1,0:T(8,128)(2,1)S(1)} all-gather(bf16[1,148,224]{2,1,0:T(8,128)(2,1)S(1)} %maximum_bitcast_fusion), channel_id=3, replica_groups=mesh['rep'=4,'dp'=8] {'dp'}, dimensions={0}, use_global_device_ids=true | all-gather | bytes 596736 | tf_op jit(solution)/shard_map/all_gather | solution.py:187
  333.0 10.9 %collective-permute-done.5 = bf16[2,224,896]{2,1,0:T(8,128)(2,1)} collective-permute-done((bf16[2,224,896]{2,1,0:T(8,128)(2,1)}, bf16[2,224,896]{2,1,0:T(8,128)(2,1)}, u32[]{:S(2)}, u32[]{:S(2)}) %collective-permute-start.5) | collective-permute-done | bytes 802848 | tf_op jit(solution)/shard_map/ppermute | solution.py:105
  346.0 14.2 %collective-permute-done.6 = bf16[2,224,896]{2,1,0:T(8,128)(2,1)} collective-permute-done((bf16[2,224,896]{2,1,0:T(8,128)(2,1)}, bf16[2,224,896]{2,1,0:T(8,128)(2,1)}, u32[]{:S(2)}, u32[]{:S(2)}) %collective-permute-start.6) | collective-permute-done | bytes 802848 | tf_op jit(solution)/shard_map/ppermute | solution.py:105
  365.3 49.6 %all_gather.60 = bf16[8,192,224]{2,1,0:T(8,128)(2,1)S(1)} all-gather(bf16[1,192,224]{2,1,0:T(8,128)(2,1)S(1)} %fusion.90), channel_id=1, replica_groups=mesh['rep'=4,'dp'=8] {'dp'}, dimensions={0}, use_global_device_ids=true | all-gather | bytes 774144 | tf_op jit(solution)/shard_map/all_gather | solution.py:52
  457.3 15.8 %all_gather.63 = bf16[192,1792]{1,0:T(8,128)(2,1)S(1)} all-gather(bf16[24,1792]{1,0:T(8,128)(2,1)S(1)} %reduce_sum.417), channel_id=1, replica_groups=mesh['rep'=4,'dp'=8] {'dp'}, dimensions={0}, use_global_device_ids=true | all-gather | bytes 774144 | tf_op jit(solution)/shard_map/all_gather | solution.py:48
  483.2 5.0 all-to-all-start.5
  491.6 21.7 %all-to-all-done.5 = bf16[8,24,1792]{2,1,0:T(8,128)(2,1)S(1)} async-done(((bf16[8,24,1792]{2,1,0:T(8,128)(2,1)}), bf16[8,24,1792]{2,1,0:T(8,128)(2,1)S(1)}, u32[]{:S(2)}, u32[]{:S(2)}) %all-to-all-start.5) | async-done | bytes 688160 | tf_op jit(solution)/shard_map/all_to_all | solution.py:59
  513.5 19.1 %all_gather.64 = bf16[192,1792]{1,0:T(8,128)(2,1)S(1)} all-gather(bf16[24,1792]{1,0:T(8,128)(2,1)S(1)} %reduce_sum.428), channel_id=1, replica_groups=mesh['rep'=4,'dp'=8] {'dp'}, dimensions={0}, use_global_device_ids=true | all-gather | bytes 774144 | tf_op jit(solution)/shard_map/all_gather | solution.py:48
  537.8 19.9 %all-gather.2 = bf16[1536,224]{1,0:T(8,128)(2,1)S(1)} all-gather(bf16[192,224]{1,0:T(8,128)(2,1)S(1)} %convolution_convert_fusion.11), channel_id=4, replica_groups=mesh['rep'=4,'dp'=8] {'dp'}, dimensions={0}, use_global_device_ids=true | all-gather | bytes 774144 | tf_op jit(solution)/shard_map/all_gather | solution.py:52
  568.4 4.3 all-to-all-start.6
  593.6 10.6 %all-to-all-done.6 = bf16[8,2,168,156]{2,1,3,0:T(2,128)(2,1)} async-done(((bf16[8,2,168,156]{2,1,3,0:T(2,128)(2,1)}), bf16[8,2,168,156]{2,1,3,0:T(2,128)(2,1)}, u32[]{:S(2)}, u32[]{:S(2)}) %all-to-all-start.6) | async-done | bytes 838688 | tf_op jit(solution)/shard_map/all_to_all | solution.py:59
  607.6 18.2 %all_gather.67 = bf16[16,168,156]{1,2,0:T(8,128)(2,1)S(1)} all-gather(bf16[2,168,156]{1,2,0:T(8,128)(2,1)S(1)} %copy.447), channel_id=1, replica_groups=mesh['rep'=4,'dp'=8] {'dp'}, dimensions={0}, use_global_device_ids=true | all-gather | bytes 943488 | tf_op jit(solution)/shard_map/all_gather | solution.py:48
  657.5 15.3 %all_gather.68 = bf16[192,1792]{1,0:T(8,128)(2,1)S(1)} all-gather(bf16[24,1792]{1,0:T(8,128)(2,1)S(1)} %reduce_sum.433), channel_id=1, replica_groups=mesh['rep'=4,'dp'=8] {'dp'}, dimensions={0}, use_global_device_ids=true | all-gather | bytes 774144 | tf_op jit(solution)/shard_map/all_gather | solution.py:48
  700.7 14.3 %all-gather.7 = f32[8,2,2496]{2,1,0:T(2,128)S(1)} all-gather(f32[1,2,2496]{2,1,0:T(2,128)S(1)} %maximum_bitcast_fusion.2), channel_id=6, replica_groups=mesh['rep'=4,'dp'=8] {'dp'}, dimensions={0}, use_global_device_ids=true | all-gather | bytes 179712 | tf_op jit(solution)/shard_map/all_gather | solution.py:339
  724.2 5.7 copy.584
  745.8 17.5 %psum.42 = f32[]{:T(128)} all-reduce(f32[]{:T(128)S(6)} %add.498), channel_id=1, replica_groups=mesh['rep'=4,'dp'=8] {'dp'}, use_global_device_ids=true, to_apply=%region_45.46 | all-reduce | flops 1 | bytes 8 | tf_op jit(solution)/shard_map/psum | solution.py:350
  765.8 25.4 %fusion.7 = bf16[2,224,7168]{2,1,0:T(8,128)(2,1)} fusion(f32[1,2,224,7168]{3,2,1,0:T(8,128)} %param.46, f32[1,2,224,7168]{3,2,1,0:T(8,128)} %param.48, f32[1,2,224,7168]{3,2,1,0:T(8,128)} %param.47, f32[1,224,7168]{2,1,0:T(8,128)} %bitcast.292, f32[1,224,7168]{2,1,0:T(8,128)} %bitcast.297, f32[]{:T(128)} %bitcast.71, f32[]{:T(128)} %bitcast.69, ...), kind=kLoop, calls=%fused_computation.14 | loop fusion | flops 61014016 | bytes 70647824 | tf_op jit(solution)/shard_map/convert_element_type | solution.py:365
  791.3 12.3 %fusion.15 = bf16[4,224,1792]{2,1,0:T(8,128)(2,1)} fusion(f32[1,4,224,1792]{3,2,1,0:T(8,128)} %param.41, f32[1,4,224,1792]{3,2,1,0:T(8,128)} %param.43, f32[1,4,224,1792]{3,2,1,0:T(8,128)} %param.42, f32[1,224,1792]{2,1,0:T(8,128)S(1)} %bitcast.302, f32[1,224,1792]{2,1,0:T(8,128)S(1)} %copy-done.16, f32[1,224,1792]{2,1,0:T(8,128)S(1)} %copy-done.17, ...), kind=kLoop, calls=%fused_computation.34 | loop fusion | flops 33718272 | bytes 35323916 | tf_op jit(solution)/shard_map/convert_element_type | solution.py:365
  814.4 13.1 %fusion.14 = (f32[1,4,224,1792]{3,2,1,0:T(8,128)}, f32[1,4,224,1792]{3,2,1,0:T(8,128)}) fusion(f32[1,4,224,1792]{3,2,1,0:T(8,128)} %param.43, f32[1,1,224,1792]{3,2,1,0:T(8,128)S(1)} %bitcast.303, f32[1,1,224,1792]{3,2,1,0:T(8,128)} %stack.142, f32[1,1,224,1792]{3,2,1,0:T(8,128)} %stack.141, f32[1,1,224,1792]{3,2,1,0:T(8,128)} %bitcast.305, f32[]{:T(128)S(6)} %div.212, ...), kind=kLoop, calls=%fused_computation.28 | loop fusion | flops 17661952 | bytes 32112644 | tf_op jit(solution)/shard_map/add | solution.py:360
  830.1 17.9 %fusion.6 = (f32[1,2,224,7168]{3,2,1,0:T(8,128)}, f32[1,2,224,7168]{3,2,1,0:T(8,128)}) fusion(f32[1,2,224,7168]{3,2,1,0:T(8,128)} %param.48, f32[1,1,224,7168]{3,2,1,0:T(8,128)S(1)} %bitcast.295, f32[1,1,224,7168]{3,2,1,0:T(8,128)S(1)} %bitcast.300, f32[]{:T(128)S(6)} %div.212, f32[1,2,224,7168]{3,2,1,0:T(8,128)} %param.47), kind=kLoop, calls=%fused_computation.8 | loop fusion | flops 28901376 | bytes 64225284 | tf_op jit(solution)/shard_map/add | solution.py:360
  851.0 157.5 %all-reduce.10.cloned.1.call-done = (bf16[4,224,1792]{2,1,0:T(8,128)(2,1)}, bf16[2,224,7168]{2,1,0:T(8,128)(2,1)}, bf16[494,224]{0,1:T(8,128)(2,1)}) async-done(((bf16[4,224,1792]{2,1,0:T(8,128)(2,1)}, bf16[2,224,7168]{2,1,0:T(8,128)(2,1)}, bf16[494,224]{0,1:T(8,128)(2,1)}), (bf16[4,224,1792]{2,1,0:T(8,128)(2,1)}, bf16[2,224,7168]{2,1,0:T(8,128)(2,1)}, ...) | async-done | bytes 9855120 | tf_op jit(solution)/shard_map/psum | solution.py:368
  1008.5 18.8 %multiply_subtract_fusion = (f32[2,224,7168]{2,1,0:T(8,128)}, f32[2,224,7168]{2,1,0:T(8,128)}) fusion(f32[2,224,7168]{2,1,0:T(8,128)} %param.45, bf16[2,224,7168]{2,1,0:T(8,128)(2,1)} %get-tuple-element.203, f32[2,224,7168]{2,1,0:T(8,128)} %param.49), kind=kLoop, calls=%fused_computation.16 | loop fusion | flops 25690112 | bytes 57802752 | tf_op jit(solution)/shard_map/sub | solution.py:374
  1027.4 8.5 multiply_subtract_fusion.1
  (480 shorter events, 314.6 us)
Async XLA Ops:
  74.1 23.1 %all-to-all-start = ((bf16[8,24,1792]{2,1,0:T(8,128)(2,1)}), bf16[8,24,1792]{2,1,0:T(8,128)(2,1)}, u32[]{:S(2)}, u32[]{:S(2)}) async-start(bf16[8,24,1792]{2,1,0:T(8,128)(2,1)} %bitcast.14), calls=%async_computation | async-start | bytes 1376256 | tf_op jit(solution)/shard_map/all_to_all | solution.py:59
  85.0 31.5 %copy-start.38 = (bf16[224,14,128]{2,1,0:T(8,128)(2,1)}, bf16[224,14,128]{2,1,0:T(8,128)(2,1)S(1)}, u32[]{:S(2)}) copy-start(bf16[224,14,128]{2,1,0:T(8,128)(2,1)S(1)} %reshape_unstack.7) | copy-start | bytes 2408452
  120.7 35.8 %all-to-all-start.1 = ((bf16[8,2,168,156]{2,1,3,0:T(2,128)(2,1)}), bf16[8,2,168,156]{2,1,3,0:T(2,128)(2,1)}, u32[]{:S(2)}, u32[]{:S(2)}) async-start(bf16[8,2,168,156]{2,1,3,0:T(2,128)(2,1)} %copy.427), calls=%async_computation.1 | async-start | bytes 2555904 | tf_op jit(solution)/shard_map/all_to_all | solution.py:59
  125.3 34.3 %copy-start.53 = (pred[168,156]{0,1:T(8,128)(4,1)}, pred[168,156]{0,1:T(8,128)(4,1)S(1)}, u32[]{:S(2)}) copy-start(pred[168,156]{0,1:T(8,128)(4,1)S(1)} %copy.419) | copy-start | bytes 78628
  127.1 54.4 %copy-start.40 = (bf16[224,14,128]{2,1,0:T(8,128)(2,1)}, bf16[224,14,128]{2,1,0:T(8,128)(2,1)S(1)}, u32[]{:S(2)}) copy-start(bf16[224,14,128]{2,1,0:T(8,128)(2,1)S(1)} %reshape_unstack.6) | copy-start | bytes 2408452
  187.9 111.1 %all-to-all-start.2 = ((bf16[8,192,224]{2,1,0:T(8,128)(2,1)}), bf16[8,192,224]{2,1,0:T(8,128)(2,1)S(1)}, u32[]{:S(2)}, u32[]{:S(2)}) async-start(bf16[8,192,224]{2,1,0:T(8,128)(2,1)} %copy.434), calls=%async_computation.2 | async-start | bytes 1572864 | tf_op jit(solution)/shard_map/all_to_all | solution.py:66
  211.4 98.8 %collective-permute-start = (bf16[2,224,896]{2,1,0:T(8,128)(2,1)}, bf16[2,224,896]{2,1,0:T(8,128)(2,1)}, u32[]{:S(2)}, u32[]{:S(2)}) collective-permute-start(bf16[2,224,896]{2,1,0:T(8,128)(2,1)} %get-tuple-element.232), channel_id=1, source_target_pairs={{0,1},{1,0},{2,3},{3,2},{4,5},{5,4},{6,7},{7,6},{8,9},{9,8},{10,11... | collective-permute-start | bytes 2408456 | tf_op jit(solution)/shard_map/ppermute | solution.py:105
  211.8 102.1 %collective-permute-start.1 = (bf16[2,224,896]{2,1,0:T(8,128)(2,1)}, bf16[2,224,896]{2,1,0:T(8,128)(2,1)}, u32[]{:S(2)}, u32[]{:S(2)}) collective-permute-start(bf16[2,224,896]{2,1,0:T(8,128)(2,1)} %get-tuple-element.231), channel_id=1, source_target_pairs={{0,2},{1,3},{2,0},{3,1},{4,6},{5,7},{6,4},{7,5},{8,10},{9,11},{10,... | collective-permute-start | bytes 2408456 | tf_op jit(solution)/shard_map/ppermute | solution.py:105
  213.5 113.2 %collective-permute-start.2 = (bf16[2,224,896]{2,1,0:T(8,128)(2,1)}, bf16[2,224,896]{2,1,0:T(8,128)(2,1)}, u32[]{:S(2)}, u32[]{:S(2)}) collective-permute-start(bf16[2,224,896]{2,1,0:T(8,128)(2,1)} %get-tuple-element.230), channel_id=1, source_target_pairs={{0,3},{1,2},{2,1},{3,0},{4,7},{5,6},{6,5},{7,4},{8,11},{9,10},{10,... | collective-permute-start | bytes 2408456 | tf_op jit(solution)/shard_map/ppermute | solution.py:105
  213.5 115.3 %collective-permute-start.3 = (bf16[2,224,896]{2,1,0:T(8,128)(2,1)}, bf16[2,224,896]{2,1,0:T(8,128)(2,1)}, u32[]{:S(2)}, u32[]{:S(2)}) collective-permute-start(bf16[2,224,896]{2,1,0:T(8,128)(2,1)} %get-tuple-element.229), channel_id=1, source_target_pairs={{0,4},{1,5},{2,6},{3,7},{4,0},{5,1},{6,2},{7,3},{8,12},{9,13},{10,... | collective-permute-start | bytes 2408456 | tf_op jit(solution)/shard_map/ppermute | solution.py:105
  216.1 114.8 %collective-permute-start.4 = (bf16[2,224,896]{2,1,0:T(8,128)(2,1)}, bf16[2,224,896]{2,1,0:T(8,128)(2,1)}, u32[]{:S(2)}, u32[]{:S(2)}) collective-permute-start(bf16[2,224,896]{2,1,0:T(8,128)(2,1)} %get-tuple-element.228), channel_id=1, source_target_pairs={{0,5},{1,4},{2,7},{3,6},{4,1},{5,0},{6,3},{7,2},{8,13},{9,12},{10,... | collective-permute-start | bytes 2408456 | tf_op jit(solution)/shard_map/ppermute | solution.py:105
  304.9 59.3 %all-to-all-start.3 = ((bf16[8,192,224]{2,1,0:T(8,128)(2,1)}), bf16[8,192,224]{2,1,0:T(8,128)(2,1)S(1)}, u32[]{:S(2)}, u32[]{:S(2)}) async-start(bf16[8,192,224]{2,1,0:T(8,128)(2,1)} %bitcast.290), calls=%async_computation.3 | async-start | bytes 1572864 | tf_op jit(solution)/shard_map/all_to_all | solution.py:66
  310.2 33.7 %collective-permute-start.5 = (bf16[2,224,896]{2,1,0:T(8,128)(2,1)}, bf16[2,224,896]{2,1,0:T(8,128)(2,1)}, u32[]{:S(2)}, u32[]{:S(2)}) collective-permute-start(bf16[2,224,896]{2,1,0:T(8,128)(2,1)} %get-tuple-element.227), channel_id=1, source_target_pairs={{0,6},{1,7},{2,4},{3,5},{4,2},{5,3},{6,0},{7,1},{8,14},{9,15},{10,... | collective-permute-start | bytes 2408456 | tf_op jit(solution)/shard_map/ppermute | solution.py:105
  314.0 46.2 %collective-permute-start.6 = (bf16[2,224,896]{2,1,0:T(8,128)(2,1)}, bf16[2,224,896]{2,1,0:T(8,128)(2,1)}, u32[]{:S(2)}, u32[]{:S(2)}) collective-permute-start(bf16[2,224,896]{2,1,0:T(8,128)(2,1)} %get-tuple-element.226), channel_id=1, source_target_pairs={{0,7},{1,6},{2,5},{3,4},{4,3},{5,2},{6,1},{7,0},{8,15},{9,14},{10,... | collective-permute-start | bytes 2408456 | tf_op jit(solution)/shard_map/ppermute | solution.py:105
  427.2 28.8 %all-to-all-start.4 = ((bf16[8,24,1792]{2,1,0:T(8,128)(2,1)}), bf16[8,24,1792]{2,1,0:T(8,128)(2,1)}, u32[]{:S(2)}, u32[]{:S(2)}) async-start(bf16[8,24,1792]{2,1,0:T(8,128)(2,1)} %bitcast.336), calls=%async_computation.4 | async-start | bytes 1376256 | tf_op jit(solution)/shard_map/all_to_all | solution.py:59
  483.2 30.1 %all-to-all-start.5 = ((bf16[8,24,1792]{2,1,0:T(8,128)(2,1)}), bf16[8,24,1792]{2,1,0:T(8,128)(2,1)S(1)}, u32[]{:S(2)}, u32[]{:S(2)}) async-start(bf16[8,24,1792]{2,1,0:T(8,128)(2,1)} %bitcast.337), calls=%async_computation.5 | async-start | bytes 1376256 | tf_op jit(solution)/shard_map/all_to_all | solution.py:59
  488.2 44.3 %copy-start.82 = (f32[192]{0:T(256)S(1)}, f32[192]{0:T(256)}, u32[]{:S(2)}) copy-start(f32[192]{0:T(256)} %copy-done.81) | copy-start | bytes 2308
  488.2 44.3 %copy-start.84 = (f32[192]{0:T(256)S(1)}, f32[192]{0:T(256)}, u32[]{:S(2)}) copy-start(f32[192]{0:T(256)} %copy-done.83) | copy-start | bytes 2308
  488.3 236.0 %all-gather.10.cloned.1.call-start = ((), (), s32[]{:S(2)}) async-start(), calls=%async_computation.8 | async-start | bytes 6193152 | tf_op jit(solution)/shard_map/all_gather | solution.py:297
  568.4 35.8 %all-to-all-start.6 = ((bf16[8,2,168,156]{2,1,3,0:T(2,128)(2,1)}), bf16[8,2,168,156]{2,1,3,0:T(2,128)(2,1)}, u32[]{:S(2)}, u32[]{:S(2)}) async-start(bf16[8,2,168,156]{2,1,3,0:T(2,128)(2,1)} %copy.446), calls=%async_computation.6 | async-start | bytes 2555904 | tf_op jit(solution)/shard_map/all_to_all | solution.py:59
  633.2 23.1 %all-to-all-start.7 = ((bf16[8,24,1792]{2,1,0:T(8,128)(2,1)}), bf16[8,24,1792]{2,1,0:T(8,128)(2,1)}, u32[]{:S(2)}, u32[]{:S(2)}) async-start(bf16[8,24,1792]{2,1,0:T(8,128)(2,1)} %convert_element_type.321), calls=%async_computation.7 | async-start | bytes 1376256 | tf_op jit(solution)/shard_map/all_to_all | solution.py:59
  637.4 210.7 %all-reduce.8.cloned.1.call-start = ((), (), s32[]{:S(2)}) async-start(), calls=%async_computation.9 | async-start | bytes 155648 | tf_op jit(solution)/shard_map/psum | solution.py:368
  738.5 25.5 %copy-start.77 = (f32[1,6,224]{2,0,1:T(1,128)S(1)}, f32[1,6,224]{2,0,1:T(1,128)}, u32[]{:S(2)}) copy-start(f32[1,6,224]{2,0,1:T(1,128)} %param.63) | copy-start | bytes 16132
  738.6 25.5 %copy-start.78 = (f32[1,6,224]{2,0,1:T(1,128)S(1)}, f32[1,6,224]{2,0,1:T(1,128)}, u32[]{:S(2)}) copy-start(f32[1,6,224]{2,0,1:T(1,128)} %param.62) | copy-start | bytes 16132
  738.6 25.5 %copy-start.80 = (f32[1,6,224]{2,0,1:T(1,128)S(1)}, f32[1,6,224]{2,0,1:T(1,128)}, u32[]{:S(2)}) copy-start(f32[1,6,224]{2,0,1:T(1,128)} %param.61) | copy-start | bytes 16132
  738.6 26.1 %copy-start.46 = (f32[142,224]{1,0:T(8,128)S(1)}, f32[142,224]{1,0:T(8,128)}, u32[]{:S(2)}) copy-start(f32[142,224]{1,0:T(8,128)} %param.55) | copy-start | bytes 381700
  738.6 26.1 %copy-start.55 = (f32[1,142,224]{2,0,1:T(1,128)S(1)}, f32[1,142,224]{2,0,1:T(1,128)}, u32[]{:S(2)}) copy-start(f32[1,142,224]{2,0,1:T(1,128)} %param.56) | copy-start | bytes 381700
  738.6 26.1 %copy-start.62 = (f32[142,224]{1,0:T(8,128)S(1)}, f32[142,224]{1,0:T(8,128)}, u32[]{:S(2)}) copy-start(f32[142,224]{1,0:T(8,128)} %get-tuple-element.260) | copy-start | bytes 381700
  738.6 26.1 %copy-start.65 = (f32[1,142,224]{2,0,1:T(1,128)S(1)}, f32[1,142,224]{2,0,1:T(1,128)}, u32[]{:S(2)}) copy-start(f32[1,142,224]{2,0,1:T(1,128)} %param.58) | copy-start | bytes 381700
  738.6 26.1 %copy-start.66 = (f32[1,142,224]{2,0,1:T(1,128)S(1)}, f32[1,142,224]{2,0,1:T(1,128)}, u32[]{:S(2)}) copy-start(f32[1,142,224]{2,0,1:T(1,128)} %param.57) | copy-start | bytes 381700
  765.5 25.8 %copy-start.9 = (f32[224,1792]{1,0:T(8,128)S(1)}, f32[224,1792]{1,0:T(8,128)}, u32[]{:S(2)}) copy-start(f32[224,1792]{1,0:T(8,128)} %fusion.83) | copy-start | bytes 4816900
  765.5 243.0 %all-reduce.10.cloned.1.call-start = ((), (), s32[]{:S(2)}) async-start(), calls=%async_computation.10 | async-start | bytes 19726336 | tf_op jit(solution)/shard_map/psum | solution.py:368
  (94 other events, 658.1 us)
Sparse Core Ops, SparseCore 0:
  491.8 73.2 all-gather.9
  765.6 39.3 all-reduce.7
  810.6 197.8 all-reduce.9

commit v2 on v1

v2 whole, which is shorter than its diff:
```python
import jax
import jax.numpy as jnp
from jax import lax
from jax.experimental import pallas as pl
from jax.experimental.pallas import tpu as pltpu
from jax.sharding import PartitionSpec as P

D = 1792
FF = 7168
HEADS = 14
HEAD_DIM = 128
PATCH_PIXELS = 196
RETURN_BINS = 120
ACTION_BINS = 18
PATCHES = 36
TIMESTEPS = 4
SPAN = 39
LENGTH = 156
PADDED = 160
HEAD_ROWS = 142
PICKS = 3 * TIMESTEPS

EPS_NORM = 1e-05
BETA_ONE = 0.9
BETA_TWO = 0.95
ADAM_EPS = 1e-08
CLIP = 1.0
OUTER_MOMENTUM = 0.9
OUTER_RATE = 0.7
RATES = (0.05, 0.05, 0.3, 0.1, 0.4)
DECAYS = (0.1, 0.1, 0.0, 0.1, 0.0)
NEGATIVE = -1e30
SCALE = 1.0 / HEAD_DIM**0.5
F32 = jnp.float32
BF16 = jnp.bfloat16


def dot(spec, left, right):
    return jnp.einsum(spec, left, right, preferred_element_type=F32)


def gelu(values):
    return (
        0.5
        * values
        * (1.0 + jnp.tanh(0.7978845608028654 * (values + 0.044715 * values * values * values)))
    )


def swap(value, step, axis="dp"):
    return lax.ppermute(value, axis, [(i, i ^ step) for i in range(lax.axis_size(axis))])


def chips():
    return lax.axis_size("dp") // 2


def still(value):
    return value


def gather_rows(piece, then=still):
    others = then([swap(piece, 2 * k) for k in range(1, chips())])
    same = jnp.concatenate([piece] + others, axis=0)
    return jnp.concatenate([same, swap(same, 1)], axis=0)


def scatter_rows(partial, then=still):
    half = partial.shape[0] // 2
    size = half // chips()
    pair = partial[:half] + swap(partial[half:].astype(BF16), 1).astype(F32)
    away = pair[size:].astype(BF16)
    others = then(
        [swap(away[(k - 1) * size : k * size], 2 * k) for k in range(1, chips())]
    )
    return sum((other.astype(F32) for other in others), pair[:size])


def sum_rows(partial, then=still):
    return gather_rows(scatter_rows(partial).astype(BF16), then)


def turn(values, step):
    count = lax.axis_size("dp")
    order = [2 * k for k in range(chips())] + [2 * k + 1 for k in range(chips())]
    bits = count.bit_length() - 1
    grid = values.reshape((2,) * bits + values.shape[1:])
    place = order.index(step)
    axes = [bits - 1 - b for b in range(bits) if place >> b & 1]
    return lax.rev(grid, axes).reshape(values.shape) if axes else values


def natural(values):
    count = lax.axis_size("dp")
    bits = count.bit_length() - 1
    here = lax.axis_index("dp")
    grid = values.reshape((2,) * bits + values.shape[1:])
    for b in range(bits - 1):
        axis = bits - 1 - b
        grid = jnp.where((here >> (b + 1)) & 1 == 1, lax.rev(grid, (axis,)), grid)
    grid = jnp.where(here & 1 == 1, lax.rev(grid, (0,)), grid)
    half = count // 2
    grid = grid.reshape((2, half) + values.shape[1:])
    return jnp.swapaxes(grid, 0, 1).reshape(values.shape)


def relative(values):
    count = lax.axis_size("dp")
    bits = count.bit_length() - 1
    here = lax.axis_index("dp")
    half = count // 2
    grid = values.reshape((half, 2) + values.shape[1:])
    grid = jnp.swapaxes(grid, 0, 1).reshape((2,) * bits + values.shape[1:])
    for b in range(bits - 1):
        axis = bits - 1 - b
        grid = jnp.where((here >> (b + 1)) & 1 == 1, lax.rev(grid, (axis,)), grid)
    grid = jnp.where(here & 1 == 1, lax.rev(grid, (0,)), grid)
    return grid.reshape(values.shape)


def split_rows(values):
    count = lax.axis_size("dp")
    return values.reshape((count, values.shape[0] // count) + values.shape[1:])


def gather_columns(piece, then=still):
    pieces = split_rows(piece)
    others = then([swap(pieces, 2 * k) for k in range(1, chips())])
    same = jnp.stack([pieces] + [turn(other, 2 * k + 2) for k, other in enumerate(others)])
    both = jnp.concatenate([same, turn_inner(swap(same, 1), 1)], axis=0)
    return jnp.moveaxis(natural(both), 0, 2).reshape(piece.shape[0], -1)


def turn_inner(values, step):
    return jnp.swapaxes(turn(jnp.swapaxes(values, 0, 1), step), 0, 1)


def scatter_columns(partial, then=still):
    count = lax.axis_size("dp")
    width = partial.shape[1] // count
    pieces = jnp.moveaxis(split_rows(partial).reshape(count, -1, count, width), 2, 0)
    pieces = relative(pieces.astype(BF16))
    half = chips()
    pair = pieces[:half].astype(F32) + turn_inner(swap(pieces[half:], 1), 1).astype(F32)
    away = pair[1:].astype(BF16)
    others = then([swap(away[k - 1], 2 * k) for k in range(1, half)])
    total = pair[0]
    for k, other in enumerate(others):
        total = total + turn(other, 2 * k + 2).astype(F32)
    return total.reshape(partial.shape[0], width)


def sum_tokens(values):
    count = lax.axis_size("dp")
    grid = jnp.swapaxes(values.reshape(values.shape[0], count, -1), 0, 1)
    grid = grid + turn(swap(grid, 1), 1)
    total = grid
    for k in range(1, chips()):
        total = total + turn(swap(grid, 2 * k), 2 * k)
    return jnp.swapaxes(total, 0, 1).reshape(values.shape)


def pairs(values):
    while len(values) > 1:
        values = [values[i] + values[i + 1] for i in range(0, len(values), 2)]
    return values[0]


def sum_scalar(value):
    value = value + swap(value, 1)
    return pairs([value] + [swap(value, 2 * k) for k in range(1, chips())])


def norm_tokens(mean, square, width, then=still):
    count = lax.axis_size("dp")
    grid = jnp.stack([mean, square], axis=0).reshape(2, count, -1).swapaxes(0, 1)
    other = turn(swap(grid, 1), 1)
    middle = 0.5 * (grid[:, 0] + other[:, 0])
    gap = grid[:, 0] - other[:, 0]
    square = grid[:, 1] + other[:, 1] + (0.5 * width) * gap * gap
    grid = jnp.stack([middle, square], axis=1)
    others = then([swap(grid, 2 * k) for k in range(1, chips())])
    pieces = [grid] + [turn(other, 2 * k + 2) for k, other in enumerate(others)]
    middle = sum(piece[:, 0] for piece in pieces) / chips()
    square = sum(
        piece[:, 1] + (2.0 * width) * jnp.square(piece[:, 0] - middle) for piece in pieces
    )
    return middle.reshape(-1), lax.rsqrt(square.reshape(-1) / D + EPS_NORM)


def norm_rows(values):
    centered = values - jnp.mean(values, axis=-1, keepdims=True)
    inverse = lax.rsqrt(jnp.mean(centered * centered, axis=-1, keepdims=True) + EPS_NORM)
    return centered * inverse, inverse


def norm_rows_back(scaled, inverse, gain, upstream):
    shaped = upstream * gain
    first = jnp.mean(shaped, axis=-1, keepdims=True)
    second = jnp.mean(shaped * scaled, axis=-1, keepdims=True)
    return inverse * (shaped - first - scaled * second)


def own_columns(values, width):
    return lax.dynamic_slice_in_dim(
        values, lax.axis_index("dp") * width, width, values.ndim - 1
    )


def relative_order():
    return [2 * k for k in range(chips())] + [2 * k + 1 for k in range(chips())]


PLAN = [
    [],
    [(0, 4), (0, 5), (0, 2)],
    [(0, 6)],
    [(0, 7), (0, 3), (0, 1)],
    [(1, 4)],
    [(1, 5), (1, 2)],
    [(1, 6), (1, 7), (1, 3), (1, 1)],
]


class Background:
    def __init__(self, weight, drift, plan):
        count = lax.axis_size("dp")
        steps = [(m, step) for m in (0, 1) for step in range(1, count)]
        known = [job for jobs in plan for job in jobs]
        rest = [job for job in steps if job not in known]
        self.plan = [[job for job in jobs if job in steps] for jobs in plan]
        self.plan[-1] += rest
        self.weight, self.drift = weight, drift
        self.width = weight.shape[1]
        self.piece = weight.shape[2] // count
        self.moving = []
        self.done = [((m, 0), self.block((m, 0))) for m in (0, 1)]

    def block(self, job):
        m, step = job
        first = (lax.axis_index("dp") ^ step) * self.piece
        size = (1, self.width, self.piece)
        spot = (m, 0, first)
        return (
            lax.dynamic_slice(self.weight, spot, size) + lax.dynamic_slice(self.drift, spot, size)
        )[0].astype(BF16)

    def __call__(self, value):
        jobs = self.plan.pop(0) if self.plan else []
        blocks = [self.block(job) for job in jobs]
        arrived = self.moving[:-2] if len(self.moving) > 2 else []
        staying = self.moving[len(arrived) :]
        value, self.weight, self.drift, blocks, ended = lax.optimization_barrier(
            (value, self.weight, self.drift, blocks, [block for _, block in arrived])
        )
        self.done += [(job, block) for (job, _), block in zip(arrived, ended)]
        self.moving = staying + [(job, swap(block, job[1])) for job, block in zip(jobs, blocks)]
        return value

    def result(self, matrix):
        here = lax.axis_index("dp")
        whole = jnp.zeros((D, self.piece), BF16)
        for (m, step), block in self.done + self.moving:
            if m == matrix:
                whole = lax.dynamic_update_slice_in_dim(
                    whole, block, (here ^ step) * self.width, 0
                )
        return whole


def inner_step_kernel(rate, decay, scalars, grad, moment, square, weight, drift, *rest):
    moment_out, square_out, change_out = rest[-3:]
    clipped = grad[...] * scalars[0]
    first = BETA_ONE * moment[...] + (1.0 - BETA_ONE) * clipped
    second = BETA_TWO * square[...] + (1.0 - BETA_TWO) * clipped * clipped
    moment_out[...] = first
    square_out[...] = second
    update = (first * scalars[1]) / (jnp.sqrt(second * scalars[2]) + ADAM_EPS)
    away = drift[...]
    change_out[...] = (rate * (update + decay * (weight[...] + away)) - away).astype(BF16)


def tall_rows(rows, columns):
    return next(
        size for size in (112, 56, 32, 16, 8, rows) if rows % size == 0 and size * columns <= 2**18
    )


def inner_update(scalars, grad, moment, square, weight, drift, rate, decay, matrix, before=None):
    matrices, rows, columns = weight.shape
    tall = tall_rows(rows, columns)
    block = pl.BlockSpec((1, tall, columns), lambda r: (matrix, r, 0))
    flat = pl.BlockSpec((tall, columns), lambda r: (r, 0))
    kept = list(before) if before else []
    return pl.pallas_call(
        lambda *refs: inner_step_kernel(
            rate,
            decay,
            refs[0],
            refs[1],
            *[ref.at[0] for ref in refs[2:6]],
            *[ref.at[0] for ref in refs[-3:]],
        ),
        grid=(rows // tall,),
        in_specs=[pl.BlockSpec(memory_space=pltpu.SMEM), flat]
        + [block] * 4
        + [pl.BlockSpec(memory_space=pl.ANY)] * len(kept),
        out_specs=[block, block, block if matrices > 2 else pl.BlockSpec((1, tall, columns), lambda r: (0, r, 0))],
        out_shape=[
            jax.ShapeDtypeStruct(weight.shape, F32),
            jax.ShapeDtypeStruct(weight.shape, F32),
            jax.ShapeDtypeStruct((matrices if matrices > 2 else 1, rows, columns), BF16),
        ],
        input_output_aliases={6 + place: place for place in range(len(kept))},
    )(scalars, grad, moment, square, weight, drift, *kept)


def outer_step_kernel(delta, velocity, weight, *rest):
    updated_out, velocity_out = rest[-2:]
    change = delta[...].astype(F32)
    speed = OUTER_MOMENTUM * velocity[...] + change
    velocity_out[...] = speed
    updated_out[...] = weight[...] - OUTER_RATE * (change + OUTER_MOMENTUM * speed)


def outer_update(delta, velocity, weight, first, before=None):
    matrices, rows, columns = delta.shape
    tall = tall_rows(rows, columns)
    block = pl.BlockSpec((1, tall, columns), lambda m, r: (m + first, r, 0))
    own = pl.BlockSpec((1, tall, columns), lambda m, r: (m, r, 0))
    kept = list(before) if before else []
    return pl.pallas_call(
        outer_step_kernel,
        grid=(matrices, rows // tall),
        in_specs=[own, block, block] + [pl.BlockSpec(memory_space=pl.ANY)] * len(kept),
        out_specs=[block, block],
        out_shape=[jax.ShapeDtypeStruct(weight.shape, F32)] * 2,
        input_output_aliases={3: 0, 4: 1} if kept else {},
    )(delta, velocity, weight, *kept)


def halve(values, axis, bit):
    size = values.shape[axis] // 2
    keep = lax.dynamic_slice_in_dim(values, bit * size, size, axis)
    give = lax.dynamic_slice_in_dim(values, (1 - bit) * size, size, axis)
    return keep, give


def join(own, other, axis, bit):
    return jnp.where(
        bit == 1,
        jnp.concatenate([other, own], axis=axis),
        jnp.concatenate([own, other], axis=axis),
    )


def mean_over_replicas(values, axis, steps):
    place = lax.axis_index("rep")
    current = values
    bits = [(place // step) % 2 for step in steps]
    for step, bit in zip(steps, bits):
        keep, give = halve(current, axis, bit)
        current = keep.astype(F32) + swap(give.astype(BF16), step, "rep").astype(F32)
    current = (current / lax.axis_size("rep")).astype(BF16)
    for step, bit in zip(reversed(steps), reversed(bits)):
        current = join(current, swap(current, step, "rep"), axis, bit)
    return current


def both_ways(values, axis, cut, steps):
    half = values.shape[cut] // 2
    first = lax.slice_in_dim(values, 0, half, axis=cut)
    second = lax.slice_in_dim(values, half, 2 * half, axis=cut)
    return jnp.concatenate(
        [mean_over_replicas(first, axis, steps), mean_over_replicas(second, axis, steps[::-1])],
        axis=cut,
    )


def shards(
    pixels,
    return_ids,
    action_ids,
    reward_ids,
    type_map,
    expert_flags,
    inner_step,
    attention_weight,
    attention_drift,
    attention_moment,
    attention_square,
    attention_velocity,
    feedforward_weight,
    feedforward_drift,
    feedforward_moment,
    feedforward_square,
    feedforward_velocity,
    embedding_weight,
    embedding_drift,
    embedding_moment,
    embedding_square,
    embedding_velocity,
    readout_weight,
    readout_drift,
    readout_moment,
    readout_square,
    readout_velocity,
    gains_weight,
    gains_drift,
    gains_moment,
    gains_square,
    gains_velocity,
):
    shared = (attention_weight, feedforward_weight, embedding_weight, readout_weight, gains_weight)
    drifts = (attention_drift, feedforward_drift, embedding_drift, readout_drift, gains_drift)
    moments = (attention_moment, feedforward_moment, embedding_moment, readout_moment, gains_moment)
    squares_old = (
        attention_square,
        feedforward_square,
        embedding_square,
        readout_square,
        gains_square,
    )
    velocities = (
        attention_velocity,
        feedforward_velocity,
        embedding_velocity,
        readout_velocity,
        gains_velocity,
    )
    attention_low, embedding_low, readout_low, gains_low = (
        (shared[group] + drifts[group][0]).astype(BF16) for group in (0, 2, 3, 4)
    )
    count = pixels.shape[0]
    devices = lax.axis_size("dp")
    seqs = count * devices
    width = D // devices
    rows = seqs * PICKS
    here = lax.axis_index("dp")

    lanes = 2 * HEAD_DIM
    pixel_rows = (pixels.astype(F32) / 127.5 - 1.0).astype(BF16)
    targets = jnp.stack(
        [return_ids, action_ids + RETURN_BINS, reward_ids + RETURN_BINS + ACTION_BINS], axis=-1
    )
    marks = (
        type_map.reshape(count, TIMESTEPS, SPAN)[:, :, PATCHES - 1 : PATCHES + 2]
        == jnp.arange(1, 4, dtype=jnp.int32)
    ).astype(F32)
    boost = jnp.array([2.0, 0.0, 0.0], dtype=F32)
    weights = marks * (1.0 + boost * expert_flags.astype(F32)[:, None, None])
    labels = jnp.stack([targets.astype(BF16), weights.astype(BF16)], axis=-1)
    labels = jnp.pad(labels, ((0, 0), (0, 0), (0, 0), (PATCH_PIXELS, lanes - PATCH_PIXELS - 2)))
    pixel_rows = jnp.pad(pixel_rows, ((0, 0), (0, 0), (0, lanes - PATCH_PIXELS)))
    packed = jnp.concatenate(
        [pixel_rows.reshape(count, TIMESTEPS, PATCHES, lanes), labels], axis=2
    ).reshape(count, LENGTH, lanes)
    packed = jnp.pad(packed, ((0, 0), (0, PADDED - LENGTH), (0, 0)))
    background = Background(
        feedforward_weight,
        feedforward_drift[0],
        PLAN,
    )
    packed = background(packed)
    packed = gather_rows(packed, background)
    small = gather_rows(jnp.concatenate([readout_low, gains_low], axis=0)[None])
    small_full = jnp.moveaxis(natural(small), 0, 1).reshape(HEAD_ROWS + 6, D)
    readout_full = small_full[:HEAD_ROWS]
    gains_full = small_full[HEAD_ROWS:].astype(F32)
    gains_own = gains_low.astype(F32)

    labels = packed[:, :LENGTH].reshape(seqs, TIMESTEPS, SPAN, lanes)
    labels = labels[:, :, PATCHES:, PATCH_PIXELS : PATCH_PIXELS + 2]
    targets = labels[..., 0].astype(jnp.int32).reshape(rows)
    weights = labels[..., 1].astype(F32).reshape(rows)
    spots = jnp.arange(PADDED, dtype=jnp.int32)
    token_target = jnp.where(
        ((spots % SPAN >= PATCHES) & (spots < LENGTH))[None, :, None],
        packed[:, :, PATCH_PIXELS : PATCH_PIXELS + 1].astype(jnp.int32),
        -1,
    )
    table_rows = jnp.arange(HEAD_ROWS + LENGTH, dtype=jnp.int32)
    picks = (table_rows == token_target) | (table_rows - HEAD_ROWS == spots[:, None])
    picks = picks.astype(BF16).reshape(seqs * PADDED, -1)
    packed = packed.reshape(seqs * PADDED, lanes)
    patch_weight = jnp.pad(embedding_low[:PATCH_PIXELS], ((0, lanes - PATCH_PIXELS), (0, 0)))
    stream = dot("tp,pd->td", packed, patch_weight) + dot(
        "tv,vd->td", picks, embedding_low[PATCH_PIXELS:]
    )

    own_mean = jnp.mean(stream, axis=-1)
    own_square = jnp.sum(jnp.square(stream - own_mean[:, None]), axis=-1)
    mean, inverse = norm_tokens(own_mean, own_square, width, background)
    inverse = inverse[:, None]
    scaled = (stream - mean[:, None]) * inverse
    normed = (scaled * gains_own[0] + gains_own[1]).astype(BF16).reshape(seqs, PADDED, width)
    place = SPAN * (jnp.arange(PICKS) // 3) + PATCHES - 1 + jnp.arange(PICKS) % 3
    selector = (place[:, None] == spots[None, :]).astype(BF16)

    query_weight, key_weight, value_weight, output_weight = attention_low
    key_weight = key_weight.reshape(width, HEADS, HEAD_DIM)
    value_weight = value_weight.reshape(width, HEADS, HEAD_DIM)
    normed_picked = dot("jk,skd->sjd", selector, normed).astype(BF16).reshape(rows, width)
    queries = sum_rows(dot("rd,de->re", normed_picked, query_weight), background)
    queries = queries.reshape(rows, HEADS, HEAD_DIM)

    def by_sequence(values):
        grid = values.reshape(HEADS, seqs, PICKS, values.shape[-1])
        return jnp.swapaxes(grid, 0, 1).reshape(seqs, HEADS * PICKS, -1)

    def by_head(values):
        grid = values.reshape(seqs, HEADS, PICKS, values.shape[-1])
        return jnp.swapaxes(grid, 0, 1).reshape(HEADS, rows, -1)

    reach = by_sequence(dot("rhe,dhe->hrd", queries, key_weight).astype(BF16))
    scores = scatter_rows(dot("sqd,skd->sqk", reach, normed), background) * SCALE
    seen = jnp.tile(spots[None, :] <= place[:, None], (HEADS, 1))
    scores = jnp.where(seen, scores, NEGATIVE)
    expos = jnp.exp(scores - jnp.max(scores, axis=-1, keepdims=True))
    probs = expos / jnp.sum(expos, axis=-1, keepdims=True)
    probs_all = gather_rows(probs.astype(BF16), background)
    blend = by_head(dot("sqk,skd->sqd", probs_all, normed).astype(BF16))
    mixed_part = dot("hrd,dhe->rhe", blend, value_weight).reshape(rows, D)
    mixed = scatter_columns(mixed_part, background).astype(BF16)
    branch_part = dot("rd,de->re", mixed, output_weight)
    picked_stream = stream.reshape(seqs, PADDED, width)[:, :LENGTH]
    picked_stream = picked_stream.reshape(seqs, TIMESTEPS, SPAN, width)
    picked_stream = picked_stream[:, :, PATCHES - 1 : PATCHES + 2].reshape(rows, width)
    own = own_columns(branch_part, width) + picked_stream
    branch_part = lax.dynamic_update_slice_in_dim(branch_part, own, here * width, 1)
    stream_one = sum_rows(branch_part).astype(F32)
    up_weight = background.result(0)
    down_weight = background.result(1)

    scaled_one, inverse_one = norm_rows(stream_one)
    normed_two = (scaled_one * gains_full[2] + gains_full[3]).astype(BF16)
    hidden = dot("rd,df->rf", normed_two, up_weight)
    activated = gelu(hidden).astype(BF16)

    def by_device(values):
        return natural(split_rows(values))

    held = by_device(activated)

    def release(arrived):
        nonlocal held
        arrived, held = lax.optimization_barrier((arrived, held))
        return arrived

    stream_two = stream_one + sum_rows(
        dot("rf,df->rd", activated, down_weight), release
    ).astype(F32)
    activated_all = gather_rows(held[None])
    scaled_two, inverse_two = norm_rows(stream_two)
    final = (scaled_two * gains_full[4] + gains_full[5]).astype(BF16)

    kinds = jnp.arange(rows) % 3
    kind_hits = (kinds[:, None] == jnp.arange(3)[None, :]).astype(F32)
    denoms = jnp.sum(weights[:, None] * kind_hits, axis=0)
    columns = jnp.arange(HEAD_ROWS, dtype=jnp.int32)
    lower = jnp.where(kinds == 0, 0, jnp.where(kinds == 1, RETURN_BINS, RETURN_BINS + ACTION_BINS))
    upper = jnp.where(
        kinds == 0, RETURN_BINS, jnp.where(kinds == 1, RETURN_BINS + ACTION_BINS, HEAD_ROWS)
    )
    allowed = (columns[None, :] >= lower[:, None]) & (columns[None, :] < upper[:, None])
    logits = dot("rd,vd->rv", final, readout_full)
    masked = jnp.where(allowed, logits, NEGATIVE)
    highest = jnp.max(masked, axis=-1, keepdims=True)
    expos = jnp.exp(masked - highest)
    totals = jnp.sum(expos, axis=-1, keepdims=True)
    onehot = (columns[None, :] == targets[:, None]).astype(F32)
    cross = highest[:, 0] + jnp.log(totals[:, 0]) - jnp.sum(onehot * logits, axis=-1)
    scale = weights / jnp.sum(kind_hits * denoms, axis=-1)
    piece_loss = jnp.sum((scale * cross).reshape(devices, -1), axis=1)
    loss = pairs([piece_loss[i] for i in range(devices)])
    slope = (scale[:, None] * (expos / totals - onehot)).astype(BF16)
    readout_grad = dot("rv,rd->vd", slope, own_columns(final, width))
    final_grad = dot("rv,vd->rd", slope, readout_full).astype(BF16).astype(F32)

    shift_five = own_columns(jnp.sum(final_grad, axis=0), width)
    gain_five = own_columns(jnp.sum(final_grad * scaled_two, axis=0), width)
    grad_two = norm_rows_back(scaled_two, inverse_two, gains_full[4], final_grad)
    output_grad = grad_two.astype(BF16)
    activated_grad = dot("rd,df->rf", output_grad, down_weight)
    unused, gelu_pull = jax.vjp(gelu, hidden)
    hidden_grad = gelu_pull(activated_grad)[0].astype(BF16)
    held = by_device(hidden_grad)
    normed_two_grad = sum_rows(dot("rf,df->rd", hidden_grad, up_weight), release).astype(F32)
    hidden_grad_all = gather_rows(held[None])

    def unit_grad(left, pieces):
        whole = jnp.zeros((width, FF), F32)
        left = by_device(left).reshape(rows, width)
        for place, step in enumerate(relative_order()):
            piece = dot("rd,rf->df", left, pieces[place].reshape(rows, -1))
            whole = lax.dynamic_update_slice_in_dim(
                whole, piece, (here ^ step) * piece.shape[1], 1
            )
        return whole

    up_grad = unit_grad(own_columns(normed_two, width), hidden_grad_all)
    down_grad = unit_grad(own_columns(output_grad, width), activated_all)
    shift_three = own_columns(jnp.sum(normed_two_grad, axis=0), width)
    gain_three = own_columns(jnp.sum(normed_two_grad * scaled_one, axis=0), width)
    grad_one = grad_two + norm_rows_back(scaled_one, inverse_one, gains_full[2], normed_two_grad)
    branch_grad = grad_one.astype(BF16)

    output_proj_grad = dot("rd,re->de", mixed, branch_grad)
    mixed_grad = gather_columns(dot("re,de->rd", branch_grad, output_weight).astype(BF16))
    mixed_grad = mixed_grad.reshape(rows, HEADS, HEAD_DIM)
    blend_grad_heads = dot("rhe,dhe->hrd", mixed_grad, value_weight).astype(BF16)
    value_weight_grad = dot("hrd,rhe->dhe", blend, mixed_grad).reshape(width, D)
    blend_grad = by_sequence(blend_grad_heads)
    prob_grad = scatter_rows(dot("sqd,skd->sqk", blend_grad, normed))
    score_grad = probs * (prob_grad - jnp.sum(probs * prob_grad, axis=-1, keepdims=True))
    score_grad = gather_rows((score_grad * SCALE).astype(BF16))
    reach_grad = by_head(dot("sqk,skd->sqd", score_grad, normed).astype(BF16))
    query_grad = sum_rows(dot("hrd,dhe->rhe", reach_grad, key_weight).reshape(rows, D))
    key_weight_grad = dot("hrd,rhe->dhe", reach_grad, queries).reshape(width, D)
    query_weight_grad = dot("rd,re->de", normed_picked, query_grad)
    through_query = dot("re,de->rd", query_grad, query_weight).astype(BF16)

    def spread(values):
        return dot("jk,sjd->skd", selector, values.reshape(seqs, PICKS, width))

    normed_grad = (
        dot("sqk,sqd->skd", probs_all, blend_grad)
        + dot("sqk,sqd->skd", score_grad, reach)
        + spread(through_query)
    ).reshape(seqs * PADDED, width)
    shift_one = jnp.sum(normed_grad, axis=0)
    gain_one = jnp.sum(normed_grad * scaled, axis=0)
    shaped = normed_grad * gains_own[0]
    sums = jnp.stack([jnp.sum(shaped, axis=-1), jnp.sum(shaped * scaled, axis=-1)])
    sums = sum_tokens(sums)[..., None] / D
    residual = spread(own_columns(branch_grad, width)).reshape(seqs * PADDED, width)
    grad_zero = (residual + inverse * (shaped - sums[0] - scaled * sums[1])).astype(BF16)
    embedding_grad = jnp.concatenate(
        [
            dot("tp,td->pd", packed, grad_zero)[:PATCH_PIXELS],
            dot("tv,td->vd", picks, grad_zero),
        ]
    )
    gains_grad = jnp.stack([gain_one, shift_one, gain_three, shift_three, gain_five, shift_five])

    attention_grads = (query_weight_grad, key_weight_grad, value_weight_grad, output_proj_grad)
    grads = attention_grads + (up_grad, down_grad, embedding_grad, readout_grad, gains_grad)
    total_squares = sum_scalar(sum((jnp.sum(grad * grad) for grad in grads)))
    gradient_norm = jnp.sqrt(total_squares)
    factor = CLIP / jnp.maximum(gradient_norm, CLIP)
    steps = inner_step[0].astype(F32)
    bias_one = 1.0 - jnp.power(F32(BETA_ONE), steps)
    bias_two = 1.0 - jnp.power(F32(BETA_TWO), steps)
    scalars = jnp.stack([factor, 1.0 / bias_one, 1.0 / bias_two])
    new_moments, new_squares = ([None] * 5, [None] * 5)

    def small_step(group, grad):
        clipped = grad * factor
        moment = BETA_ONE * moments[group][0] + (1.0 - BETA_ONE) * clipped
        square = BETA_TWO * squares_old[group][0] + (1.0 - BETA_TWO) * clipped * clipped
        drift = drifts[group][0]
        update = moment / bias_one / (jnp.sqrt(square / bias_two) + ADAM_EPS) + DECAYS[group] * (
            shared[group] + drift
        )
        new_moments[group] = moment
        new_squares[group] = square
        return (RATES[group] * update - drift).astype(BF16)

    def big_step(group, matrix, grad, before=None):
        return inner_update(
            scalars,
            grad,
            moments[group][0],
            squares_old[group][0],
            shared[group],
            drifts[group][0],
            RATES[group],
            DECAYS[group],
            matrix,
            before,
        )

    before = None
    for matrix, grad in enumerate(attention_grads):
        before = big_step(0, matrix, grad, before)
    new_moments[0], new_squares[0], attention_change = before
    up_grad, attention_change = lax.optimization_barrier((up_grad, attention_change))
    *before, up_change = big_step(1, 0, up_grad)
    down_grad, up_change = lax.optimization_barrier((down_grad, up_change))
    new_moments[1], new_squares[1], down_change = big_step(1, 1, down_grad, before)
    replicas = lax.axis_size("rep")
    exchange = [1 << b for b in range(replicas.bit_length() - 1)]
    attention_delta = both_ways(attention_change, 0, 2, exchange)
    up_delta = both_ways(up_change, 2, 1, exchange)
    down_delta = both_ways(down_change, 2, 1, exchange)
    small_changes = jnp.concatenate(
        [small_step(2, embedding_grad), small_step(3, readout_grad), small_step(4, gains_grad)]
    )
    others = [small_changes] + [swap(small_changes, step, "rep") for step in range(1, replicas)]
    small_delta = pairs([other.astype(F32) for other in others]) / replicas

    finished = {0: outer_update(attention_delta, velocities[0], shared[0], 0)}
    before = outer_update(up_delta, velocities[1], shared[1], 0)
    finished[1] = outer_update(down_delta, velocities[1], shared[1], 1, before)
    outputs = [loss[None], gradient_norm[None]]
    bound = 0
    for group in range(5):
        if group in finished:
            updated, velocity = finished[group]
        else:
            delta = small_delta[bound : bound + shared[group].shape[0]]
            bound += shared[group].shape[0]
            velocity = OUTER_MOMENTUM * velocities[group] + delta
            updated = shared[group] - OUTER_RATE * (delta + OUTER_MOMENTUM * velocity)
        outputs.append(updated)
        outputs.append(new_moments[group][None])
        outputs.append(new_squares[group][None])
        outputs.append(velocity)
    return tuple(outputs)


def solution(mesh):
    placed = (
        P(("rep", "dp"), None, None),
        P(("rep", "dp"), None),
        P(("rep", "dp"), None),
        P(("rep", "dp"), None),
        P(("rep", "dp"), None),
        P(("rep", "dp")),
        P(),
        P(None, "dp", None),
        P("rep", None, "dp", None),
        P("rep", None, "dp", None),
        P("rep", None, "dp", None),
        P(None, "dp", None),
        P(None, "dp", None),
        P("rep", None, "dp", None),
        P("rep", None, "dp", None),
        P("rep", None, "dp", None),
        P(None, "dp", None),
        P(None, "dp"),
        P("rep", None, "dp"),
        P("rep", None, "dp"),
        P("rep", None, "dp"),
        P(None, "dp"),
        P(None, "dp"),
        P("rep", None, "dp"),
        P("rep", None, "dp"),
        P("rep", None, "dp"),
        P(None, "dp"),
        P(None, "dp"),
        P("rep", None, "dp"),
        P("rep", None, "dp"),
        P("rep", None, "dp"),
        P(None, "dp"),
    )
    return jax.shard_map(
        shards,
        mesh=mesh,
        in_specs=placed,
        out_specs=(
            P("rep"),
            P("rep"),
            P(None, "dp", None),
            P("rep", None, "dp", None),
            P("rep", None, "dp", None),
            P(None, "dp", None),
            P(None, "dp", None),
            P("rep", None, "dp", None),
            P("rep", None, "dp", None),
            P(None, "dp", None),
            P(None, "dp"),
            P("rep", None, "dp"),
            P("rep", None, "dp"),
            P(None, "dp"),
            P(None, "dp"),
            P("rep", None, "dp"),
            P("rep", None, "dp"),
            P(None, "dp"),
            P(None, "dp"),
            P("rep", None, "dp"),
            P("rep", None, "dp"),
            P(None, "dp"),
        ),
        check_vma=False,
    )
```

time: 1060 us -> 918 us (0.87)
  blocking collectives: 319 us -> 0 us
  starting transfers between devices: 42.2 us -> 189 us
  Pallas kernels: 0 us -> 93.8 us
  other arithmetic: 172 us -> 121 us
  local copies, waits for them, and re-layouts: 177 us -> 157 us
  matrix products: 53.9 us -> 71 us
    all_gather x12 -> x0, blocking collectives: 302 us -> none  [the longest x7 123 us: gather_rows(): return lax.all_gather(piece, 'dp', axis=0, tiled=True)]
    ppermute x7 -> x133, waiting for transfers between devices: 25.1 us -> 259 us  [swap(): lax.ppermute(value, axis, [(i, i ^ step) for i in range(lax.axis_size(axi...]
    ppermute x7 -> x133, starting transfers between devices: 8.53 us -> 189 us  [swap(): lax.ppermute(value, axis, [(i, i ^ step) for i in range(lax.axis_size(axi...]
    psum x2 -> x0, waiting for transfers between devices: 158 us -> none  [shards(): summed = lax.psum(tuple(changes), 'rep')]
    pallas_call x0 -> x9, Pallas kernels: none -> 93.8 us  [the longest x6 57 us: inner_update(): pl.pallas_call(lambda *refs: inner_step_kernel(rate, decay, refs[0], refs...]
    all_to_all x8 -> x0, waiting for transfers between devices: 76.6 us -> none  [the longest x6 74.7 us: scatter_rows(): mine = lax.all_to_all(parts, 'dp', split_axis=0, concat_axis=0, tiled=True)]
    all_to_all x8 -> x0, starting transfers between devices: 33.3 us -> none  [the longest x6 26.2 us: scatter_rows(): mine = lax.all_to_all(parts, 'dp', split_axis=0, concat_axis=0, tiled=True)]
    convert_element_type x16 -> x25, other arithmetic: 60.9 us -> 31.9 us  [the longest x6 18.5 us: block(): return (lax.dynamic_slice(self.weight, spot, size) + lax.dynamic_slice(se...]
  transfers between devices with their start and end apart: 18 -> 133, of which waited for: 9 -> 44; matrix products, arithmetic and copies ran while one was open for 25% -> 32% of each run, Pallas kernels for 0% -> 8%
where the time goes in v2:
time: 918 us; the launch traced here: 912 us
  waiting for transfers between devices  259 us (28%)
  starting transfers between devices  189 us (21%)
  local copies, waits for them, and re-layouts  157 us (17%)
  other arithmetic  121 us (13%)
  Pallas kernels  93.8 us (10%)
  matrix products  71 us (8%)
  between operations  21.1 us (2%)
    ppermute x133, waiting for transfers between devices, swap(): lax.ppermute(value, axis, [(i, i ^ step) for i in range(lax.axis_size(axi...  259 us
    ppermute x133, starting transfers between devices, swap(): lax.ppermute(value, axis, [(i, i ^ step) for i in range(lax.axis_size(axi...  189 us
    dot_general x48, matrix products, dot(): return jnp.einsum(spec, left, right, preferred_element_type=F32)  71 us
    pallas_call x6, Pallas kernels, inner_update(): pl.pallas_call(lambda *refs: inner_step_kernel(rate, decay, refs[0], refs...  57 us
    pallas_call x3, Pallas kernels, outer_update(): pl.pallas_call(outer_step_kernel, grid=(matrices, rows // tall), in_specs...  36.8 us
    unnamed x323, local copies, waits for them, and re-layouts  36.3 us
    convert_element_type x6, other arithmetic, block(): return (lax.dynamic_slice(self.weight, spot, size) + lax.dynamic_slice(se...  18.5 us
  transfers between devices with their start and end apart: 133, of which 44 were waited for; matrix products, arithmetic and copies ran while one was open for 32% of the time, Pallas kernels for 8%

profile of v2, /device:TPU:0, one launch (start us, length us, event | category | flops | bytes accessed | tf_op | source)
XLA Modules:
  0.0 911.8 jit_solution(974584145529958507)
XLA Ops:
  20.3 5.4 add_convert_fusion
  80.4 12.6 %collective-permute-done.8 = bf16[224,896]{1,0:T(8,128)(2,1)} collective-permute-done((bf16[224,896]{1,0:T(8,128)(2,1)}, bf16[224,896]{1,0:T(8,128)(2,1)}, u32[]{:S(2)}, u32[]{:S(2)}) %collective-permute-start.8) | collective-permute-done | bytes 401440 | tf_op jit(solution)/shard_map/ppermute | solution.py:51
  93.0 8.9 collective-permute-done.6
  180.7 21.5 %collective-permute-start.28 = (bf16[224,896]{1,0:T(8,128)(2,1)S(1)}, bf16[224,896]{1,0:T(8,128)(2,1)S(1)}, u32[]{:S(2)}, u32[]{:S(2)}) collective-permute-start(bf16[224,896]{1,0:T(8,128)(2,1)S(1)} %copy-done.93), channel_id=1, source_target_pairs={{0,3},{1,2},{2,1},{3,0},{4,7},{5,6},{6,5},{7,4},{8,11},{9,10},{10,... | collective-permute-start | bytes 1204232 | tf_op jit(solution)/shard_map/ppermute | solution.py:51
  203.8 11.5 %collective-permute-done.20 = bf16[2,168,160]{1,2,0:T(8,128)(2,1)S(1)} collective-permute-done((bf16[2,168,160]{1,2,0:T(8,128)(2,1)S(1)}, bf16[2,168,160]{1,2,0:T(8,128)(2,1)S(1)}, u32[]{:S(2)}, u32[]{:S(2)}) %collective-permute-start.20) | collective-permute-done | bytes 107552 | tf_op jit(solution)/shard_map/ppermute | solution.py:51
  225.9 16.8 %collective-permute-done.26 = bf16[2,168,160]{1,2,0:T(8,128)(2,1)S(1)} collective-permute-done((bf16[2,168,160]{1,2,0:T(8,128)(2,1)S(1)}, bf16[2,168,160]{1,2,0:T(8,128)(2,1)S(1)}, u32[]{:S(2)}, u32[]{:S(2)}) %collective-permute-start.26) | collective-permute-done | bytes 107552 | tf_op jit(solution)/shard_map/ppermute | solution.py:51
  273.2 14.3 %collective-permute-done.32 = bf16[8,24,224]{2,1,0:T(8,128)(2,1)S(1)} collective-permute-done((bf16[8,24,224]{2,1,0:T(8,128)(2,1)S(1)}, bf16[8,24,224]{2,1,0:T(8,128)(2,1)S(1)}, u32[]{:S(2)}, u32[]{:S(2)}) %collective-permute-start.32) | collective-permute-done | bytes 86048 | tf_op jit(solution)/shard_map/ppermute | solution.py:51
  303.1 11.0 %collective-permute-done.48 = bf16[224,896]{1,0:T(8,128)(2,1)} collective-permute-done((bf16[224,896]{1,0:T(8,128)(2,1)}, bf16[224,896]{1,0:T(8,128)(2,1)}, u32[]{:S(2)}, u32[]{:S(2)}) %collective-permute-start.48) | collective-permute-done | bytes 401440 | tf_op jit(solution)/shard_map/ppermute | solution.py:51
  330.4 7.1 collective-permute-done.38
  343.7 6.7 collective-permute-done.41
  363.8 6.7 collective-permute-done.56
  375.7 5.5 collective-permute-done.59
  398.2 11.3 %collective-permute-done.95 = bf16[1,8,24,896]{3,2,1,0:T(8,128)(2,1)S(1)} collective-permute-done((bf16[1,8,24,896]{3,2,1,0:T(8,128)(2,1)S(1)}, bf16[1,8,24,896]{3,2,1,0:T(8,128)(2,1)S(1)}, u32[]{:S(2)}, u32[]{:S(2)}) %collective-permute-start.95) | collective-permute-done | bytes 344096 | tf_op jit(solution)/shard_map/ppermute | solution.py:51
  423.8 6.1 collective-permute-start.63
  433.0 6.7 collective-permute-done.64
  470.9 11.3 %collective-permute-done.91 = bf16[1,8,24,896]{3,2,1,0:T(8,128)(2,1)S(1)} collective-permute-done((bf16[1,8,24,896]{3,2,1,0:T(8,128)(2,1)}, bf16[1,8,24,896]{3,2,1,0:T(8,128)(2,1)S(1)}, u32[]{:S(2)}, u32[]{:S(2)}) %collective-permute-start.91) | collective-permute-done | bytes 344096 | tf_op jit(solution)/shard_map/ppermute | solution.py:51
  536.3 8.2 collective-permute-done.76
  555.0 6.6 collective-permute-done.79
  584.8 5.8 collective-permute-done.84
  685.8 18.3 %shard_map.485 = (f32[2,224,7168]{2,1,0:T(8,128)}, f32[2,224,7168]{2,1,0:T(8,128)}, bf16[1,224,7168]{2,1,0:T(8,128)(2,1)}) custom-call(f32[3]{0:T(128)} %pad_maximum_fusion.20.refs_0_, f32[224,7168]{1,0:T(8,128)} %convolution_dynamic-update-slice_fusion.8.refs_1_, f32[2,224,7168]{2,1,0:T(8,128)} %bitcast.546, f32[2,224,7168]{2,1,0:T(8,128)} %bitcast.548, ...), custom_call_target="tpu_custom_call" | custom-call | tf_op jit(solution)/shard_map/pallas_call | solution.py:295
  711.2 18.2 %shard_map.486 = (f32[2,224,7168]{2,1,0:T(8,128)}, f32[2,224,7168]{2,1,0:T(8,128)}, bf16[1,224,7168]{2,1,0:T(8,128)(2,1)}) custom-call(f32[3]{0:T(128)} %pad_maximum_fusion.20.refs_0_, f32[224,7168]{1,0:T(8,128)} %convolution_dynamic-update-slice_fusion.refs_1_, f32[2,224,7168]{2,1,0:T(8,128)} %bitcast.547, ...), custom_call_target="tpu_custom_call", output_to_operand_aliasing={{0}: (6, {}), {1}: (7, {})} | custom-call | tf_op jit(solution)/shard_map/pallas_call | solution.py:295
  762.5 13.3 %collective-permute-done.106 = bf16[2,224,896]{2,1,0:T(8,128)(2,1)} collective-permute-done((bf16[2,224,896]{2,1,0:T(8,128)(2,1)}, bf16[2,224,896]{2,1,0:T(8,128)(2,1)}, u32[]{:S(2)}, u32[]{:S(2)}) %collective-permute-start.106) | collective-permute-done | bytes 802848 | tf_op jit(solution)/shard_map/ppermute | solution.py:51
  778.5 6.4 collective-permute-done.123
  787.0 6.5 collective-permute-done.115
  795.6 6.5 collective-permute-done.107
  804.2 6.5 collective-permute-done.124
  813.3 5.9 collective-permute-done.116
  830.7 13.8 %collective-permute-done.125 = bf16[1,112,3584]{2,1,0:T(8,128)(2,1)S(1)} collective-permute-done((bf16[1,112,3584]{2,1,0:T(8,128)(2,1)S(1)}, bf16[1,112,3584]{2,1,0:T(8,128)(2,1)S(1)}, u32[]{:S(2)}, u32[]{:S(2)}) %collective-permute-start.125) | collective-permute-done | bytes 802848 | tf_op jit(solution)/shard_map/ppermute | solution.py:51
  847.7 12.4 %shard_map.487 = (f32[2,224,7168]{2,1,0:T(8,128)}, f32[2,224,7168]{2,1,0:T(8,128)}) custom-call(bf16[1,224,7168]{2,1,0:T(8,128)(2,1)} %pad_maximum_fusion.2.delta, f32[2,224,7168]{2,1,0:T(8,128)} %velocity.5, f32[2,224,7168]{2,1,0:T(8,128)} %weight.5), custom_call_target="tpu_custom_call" | custom-call | tf_op jit(solution)/shard_map/pallas_call | solution.py:332
  860.1 14.0 %collective-permute-done.109 = bf16[2,224,896]{2,1,0:T(8,128)(2,1)} collective-permute-done((bf16[2,224,896]{2,1,0:T(8,128)(2,1)S(1)}, bf16[2,224,896]{2,1,0:T(8,128)(2,1)}, u32[]{:S(2)}, u32[]{:S(2)}) %collective-permute-start.109) | collective-permute-done | bytes 802848 | tf_op jit(solution)/shard_map/ppermute | solution.py:51
  884.9 12.0 %shard_map.484 = (f32[4,224,1792]{2,1,0:T(8,128)}, f32[4,224,1792]{2,1,0:T(8,128)}) custom-call(bf16[4,224,1792]{2,1,0:T(8,128)(2,1)} %pad_maximum_fusion.delta, f32[4,224,1792]{2,1,0:T(8,128)} %velocity.3, f32[4,224,1792]{2,1,0:T(8,128)} %weight.3), custom_call_target="tpu_custom_call" | custom-call | tf_op jit(solution)/shard_map/pallas_call | solution.py:332
  896.9 12.4 %shard_map.488 = (f32[2,224,7168]{2,1,0:T(8,128)}, f32[2,224,7168]{2,1,0:T(8,128)}) custom-call(bf16[1,224,7168]{2,1,0:T(8,128)(2,1)} %pad_maximum_fusion.1.delta, f32[2,224,7168]{2,1,0:T(8,128)} %velocity.5, f32[2,224,7168]{2,1,0:T(8,128)} %weight.5, f32[2,224,7168]{2,1,0:T(8,128)} %get-tuple-element.194.rest_0_, ...), custom_call_target="tpu_custom_call", output_to_operand_aliasing={{0}: (3, {}), {1}: (4, {})} | custom-call | tf_op jit(solution)/shard_map/pallas_call | solution.py:332
  (969 shorter events, 560.6 us)
Async XLA Ops:
  6.5 49.4 %collective-permute-start = (bf16[2,160,256]{2,1,0:T(8,128)(2,1)S(1)}, bf16[2,160,256]{2,1,0:T(8,128)(2,1)S(1)}, u32[]{:S(2)}, u32[]{:S(2)}) collective-permute-start(bf16[2,160,256]{2,1,0:T(8,128)(2,1)S(1)} %pad.18), channel_id=1, source_target_pairs={{0,2},{1,3},{2,0},{3,1},{4,6},{5,7},{6,4},{7,5},{8,10},{9,11},{10,... | collective-permute-start | bytes 491528 | tf_op jit(solution)/shard_map/ppermute | solution.py:51
  9.6 46.3 %collective-permute-start.1 = (bf16[2,160,256]{2,1,0:T(8,128)(2,1)S(1)}, bf16[2,160,256]{2,1,0:T(8,128)(2,1)}, u32[]{:S(2)}, u32[]{:S(2)}) collective-permute-start(bf16[2,160,256]{2,1,0:T(8,128)(2,1)S(1)} %pad.18), channel_id=1, source_target_pairs={{0,4},{1,5},{2,6},{3,7},{4,0},{5,1},{6,2},{7,3},{8,12},{9,13},{10,... | collective-permute-start | bytes 491528 | tf_op jit(solution)/shard_map/ppermute | solution.py:51
  12.9 39.1 %collective-permute-start.44 = (bf16[1,148,224]{2,1,0:T(8,128)(2,1)}, bf16[1,148,224]{2,1,0:T(8,128)(2,1)}, u32[]{:S(2)}, u32[]{:S(2)}) collective-permute-start(bf16[1,148,224]{2,1,0:T(8,128)(2,1)} %maximum_bitcast_fusion), channel_id=1, source_target_pairs={{0,2},{1,3},{2,0},{3,1},{4,6},{5,7},{6,4},{7,5},{8,10},{9,11},{10,... | collective-permute-start | bytes 198920 | tf_op jit(solution)/shard_map/ppermute | solution.py:51
  13.4 38.7 %collective-permute-start.45 = (bf16[1,148,224]{2,1,0:T(8,128)(2,1)}, bf16[1,148,224]{2,1,0:T(8,128)(2,1)}, u32[]{:S(2)}, u32[]{:S(2)}) collective-permute-start(bf16[1,148,224]{2,1,0:T(8,128)(2,1)} %maximum_bitcast_fusion), channel_id=1, source_target_pairs={{0,4},{1,5},{2,6},{3,7},{4,0},{5,1},{6,2},{7,3},{8,12},{9,13},{10,... | collective-permute-start | bytes 198920 | tf_op jit(solution)/shard_map/ppermute | solution.py:51
  13.4 38.7 %collective-permute-start.46 = (bf16[1,148,224]{2,1,0:T(8,128)(2,1)}, bf16[1,148,224]{2,1,0:T(8,128)(2,1)}, u32[]{:S(2)}, u32[]{:S(2)}) collective-permute-start(bf16[1,148,224]{2,1,0:T(8,128)(2,1)} %maximum_bitcast_fusion), channel_id=1, source_target_pairs={{0,6},{1,7},{2,4},{3,5},{4,2},{5,3},{6,0},{7,1},{8,14},{9,15},{10,... | collective-permute-start | bytes 198920 | tf_op jit(solution)/shard_map/ppermute | solution.py:51
  61.7 86.8 %collective-permute-start.16 = (bf16[224,896]{1,0:T(8,128)(2,1)}, bf16[224,896]{1,0:T(8,128)(2,1)}, u32[]{:S(2)}, u32[]{:S(2)}) collective-permute-start(bf16[224,896]{1,0:T(8,128)(2,1)} %get-tuple-element.125), channel_id=1, source_target_pairs={{0,5},{1,4},{2,7},{3,6},{4,1},{5,0},{6,3},{7,2},{8,13},{9,12},{10,... | collective-permute-start | bytes 1204232 | tf_op jit(solution)/shard_map/ppermute | solution.py:51
  93.0 83.4 %collective-permute-start.22 = (bf16[224,896]{1,0:T(8,128)(2,1)}, bf16[224,896]{1,0:T(8,128)(2,1)}, u32[]{:S(2)}, u32[]{:S(2)}) collective-permute-start(bf16[224,896]{1,0:T(8,128)(2,1)} %get-tuple-element.131), channel_id=1, source_target_pairs={{0,2},{1,3},{2,0},{3,1},{4,6},{5,7},{6,4},{7,5},{8,10},{9,11},{10,... | collective-permute-start | bytes 1204232 | tf_op jit(solution)/shard_map/ppermute | solution.py:51
  168.7 33.6 %collective-permute-start.24 = (bf16[224,896]{1,0:T(8,128)(2,1)}, bf16[224,896]{1,0:T(8,128)(2,1)S(1)}, u32[]{:S(2)}, u32[]{:S(2)}) collective-permute-start(bf16[224,896]{1,0:T(8,128)(2,1)} %get-tuple-element.133), channel_id=1, source_target_pairs={{0,7},{1,6},{2,5},{3,4},{4,3},{5,2},{6,1},{7,0},{8,15},{9,14},{10,... | collective-permute-start | bytes 1204232 | tf_op jit(solution)/shard_map/ppermute | solution.py:51
  174.6 40.7 %collective-permute-start.20 = (bf16[2,168,160]{1,2,0:T(8,128)(2,1)S(1)}, bf16[2,168,160]{1,2,0:T(8,128)(2,1)S(1)}, u32[]{:S(2)}, u32[]{:S(2)}) collective-permute-start(bf16[2,168,160]{1,2,0:T(8,128)(2,1)S(1)} %get-tuple-element.425), channel_id=1, source_target_pairs={{0,4},{1,5},{2,6},{3,7},{4,0},{5,1},{6,2},{7,3},{8,12},{9,13},{10,... | collective-permute-start | bytes 322568 | tf_op jit(solution)/shard_map/ppermute | solution.py:51
  176.4 38.8 %collective-permute-start.21 = (bf16[2,168,160]{1,2,0:T(8,128)(2,1)S(1)}, bf16[2,168,160]{1,2,0:T(8,128)(2,1)S(1)}, u32[]{:S(2)}, u32[]{:S(2)}) collective-permute-start(bf16[2,168,160]{1,2,0:T(8,128)(2,1)S(1)} %get-tuple-element.424), channel_id=1, source_target_pairs={{0,6},{1,7},{2,4},{3,5},{4,2},{5,3},{6,0},{7,1},{8,14},{9,15},{10,... | collective-permute-start | bytes 322568 | tf_op jit(solution)/shard_map/ppermute | solution.py:51
  180.7 44.2 %collective-permute-start.28 = (bf16[224,896]{1,0:T(8,128)(2,1)S(1)}, bf16[224,896]{1,0:T(8,128)(2,1)S(1)}, u32[]{:S(2)}, u32[]{:S(2)}) collective-permute-start(bf16[224,896]{1,0:T(8,128)(2,1)S(1)} %copy-done.93), channel_id=1, source_target_pairs={{0,3},{1,2},{2,1},{3,0},{4,7},{5,6},{6,5},{7,4},{8,11},{9,10},{10,... | collective-permute-start | bytes 1204232 | tf_op jit(solution)/shard_map/ppermute | solution.py:51
  202.3 69.3 %collective-permute-start.34 = (bf16[224,896]{1,0:T(8,128)(2,1)}, bf16[224,896]{1,0:T(8,128)(2,1)}, u32[]{:S(2)}, u32[]{:S(2)}) collective-permute-start(bf16[224,896]{1,0:T(8,128)(2,1)} %get-tuple-element.145), channel_id=1, source_target_pairs={{0,1},{1,0},{2,3},{3,2},{4,5},{5,4},{6,7},{7,6},{8,9},{9,8},{10,11... | collective-permute-start | bytes 1204232 | tf_op jit(solution)/shard_map/ppermute | solution.py:51
  225.0 47.0 %collective-permute-start.35 = (bf16[224,896]{1,0:T(8,128)(2,1)}, bf16[224,896]{1,0:T(8,128)(2,1)}, u32[]{:S(2)}, u32[]{:S(2)}) collective-permute-start(bf16[224,896]{1,0:T(8,128)(2,1)} %fusion.90), channel_id=1, source_target_pairs={{0,4},{1,5},{2,6},{3,7},{4,0},{5,1},{6,2},{7,3},{8,12},{9,13},{10,... | collective-permute-start | bytes 1204232 | tf_op jit(solution)/shard_map/ppermute | solution.py:51
  271.6 42.5 %collective-permute-start.48 = (bf16[224,896]{1,0:T(8,128)(2,1)}, bf16[224,896]{1,0:T(8,128)(2,1)}, u32[]{:S(2)}, u32[]{:S(2)}) collective-permute-start(bf16[224,896]{1,0:T(8,128)(2,1)} %get-tuple-element.158), channel_id=1, source_target_pairs={{0,5},{1,4},{2,7},{3,6},{4,1},{5,0},{6,3},{7,2},{8,13},{9,12},{10,... | collective-permute-start | bytes 1204232 | tf_op jit(solution)/shard_map/ppermute | solution.py:51
  272.0 45.2 %collective-permute-start.49 = (bf16[224,896]{1,0:T(8,128)(2,1)}, bf16[224,896]{1,0:T(8,128)(2,1)}, u32[]{:S(2)}, u32[]{:S(2)}) collective-permute-start(bf16[224,896]{1,0:T(8,128)(2,1)} %get-tuple-element.159), channel_id=1, source_target_pairs={{0,2},{1,3},{2,0},{3,1},{4,6},{5,7},{6,4},{7,5},{8,10},{9,11},{10,... | collective-permute-start | bytes 1204232 | tf_op jit(solution)/shard_map/ppermute | solution.py:51
  287.5 32.3 %collective-permute-start.50 = (bf16[224,896]{1,0:T(8,128)(2,1)}, bf16[224,896]{1,0:T(8,128)(2,1)}, u32[]{:S(2)}, u32[]{:S(2)}) collective-permute-start(bf16[224,896]{1,0:T(8,128)(2,1)} %get-tuple-element.160), channel_id=1, source_target_pairs={{0,6},{1,7},{2,4},{3,5},{4,2},{5,3},{6,0},{7,1},{8,14},{9,15},{10,... | collective-permute-start | bytes 1204232 | tf_op jit(solution)/shard_map/ppermute | solution.py:51
  289.4 36.8 %collective-permute-start.51 = (bf16[224,896]{1,0:T(8,128)(2,1)}, bf16[224,896]{1,0:T(8,128)(2,1)}, u32[]{:S(2)}, u32[]{:S(2)}) collective-permute-start(bf16[224,896]{1,0:T(8,128)(2,1)} %get-tuple-element.161), channel_id=1, source_target_pairs={{0,7},{1,6},{2,5},{3,4},{4,3},{5,2},{6,1},{7,0},{8,15},{9,14},{10,... | collective-permute-start | bytes 1204232 | tf_op jit(solution)/shard_map/ppermute | solution.py:51
  289.4 39.8 %collective-permute-start.52 = (bf16[224,896]{1,0:T(8,128)(2,1)}, bf16[224,896]{1,0:T(8,128)(2,1)}, u32[]{:S(2)}, u32[]{:S(2)}) collective-permute-start(bf16[224,896]{1,0:T(8,128)(2,1)} %get-tuple-element.162), channel_id=1, source_target_pairs={{0,3},{1,2},{2,1},{3,0},{4,7},{5,6},{6,5},{7,4},{8,11},{9,10},{10,... | collective-permute-start | bytes 1204232 | tf_op jit(solution)/shard_map/ppermute | solution.py:51
  410.8 109.5 %collective-permute-start.97 = (bf16[4,8,24,896]{3,2,1,0:T(8,128)(2,1)}, bf16[4,8,24,896]{3,2,1,0:T(8,128)(2,1)}, u32[]{:S(2)}, u32[]{:S(2)}) collective-permute-start(bf16[4,8,24,896]{3,2,1,0:T(8,128)(2,1)} %pad_maximum_fusion.4), channel_id=1, source_target_pairs={{0,1},{1,0},{2,3},{3,2},{4,5},{5,4},{6,7},{7,6},{8,9},{9,8},{10,11... | collective-permute-start | bytes 4128776 | tf_op jit(solution)/shard_map/ppermute | solution.py:51
  453.0 34.6 %collective-permute-start.92 = (bf16[1,8,24,896]{3,2,1,0:T(8,128)(2,1)}, bf16[1,8,24,896]{3,2,1,0:T(8,128)(2,1)}, u32[]{:S(2)}, u32[]{:S(2)}) collective-permute-start(bf16[1,8,24,896]{3,2,1,0:T(8,128)(2,1)} %bitcast.122), channel_id=1, source_target_pairs={{0,6},{1,7},{2,4},{3,5},{4,2},{5,3},{6,0},{7,1},{8,14},{9,15},{10,... | collective-permute-start | bytes 1032200 | tf_op jit(solution)/shard_map/ppermute | solution.py:51
  500.4 61.6 %collective-permute-start.93 = (bf16[4,8,24,896]{3,2,1,0:T(8,128)(2,1)}, bf16[4,8,24,896]{3,2,1,0:T(8,128)(2,1)}, u32[]{:S(2)}, u32[]{:S(2)}) collective-permute-start(bf16[4,8,24,896]{3,2,1,0:T(8,128)(2,1)} %pad_maximum_fusion.3), channel_id=1, source_target_pairs={{0,1},{1,0},{2,3},{3,2},{4,5},{5,4},{6,7},{7,6},{8,9},{9,8},{10,11... | collective-permute-start | bytes 4128776 | tf_op jit(solution)/shard_map/ppermute | solution.py:51
  656.2 81.2 %collective-permute-start.130 = (bf16[642,224]{1,0:T(8,128)(2,1)}, bf16[642,224]{1,0:T(8,128)(2,1)}, u32[]{:S(2)}, u32[]{:S(2)}) collective-permute-start(bf16[642,224]{1,0:T(8,128)(2,1)} %pad_maximum_fusion.15), channel_id=1, source_target_pairs={{0,8},{8,0},{16,24},{24,16},{1,9},{9,1},{17,25},{25,17},{2,10},{10... | collective-permute-start | bytes 862856 | tf_op jit(solution)/shard_map/ppermute | solution.py:51
  657.7 80.3 %collective-permute-start.131 = (bf16[642,224]{1,0:T(8,128)(2,1)}, bf16[642,224]{1,0:T(8,128)(2,1)}, u32[]{:S(2)}, u32[]{:S(2)}) collective-permute-start(bf16[642,224]{1,0:T(8,128)(2,1)} %pad_maximum_fusion.15), channel_id=1, source_target_pairs={{0,16},{8,24},{16,0},{24,8},{1,17},{9,25},{17,1},{25,9},{2,18},{10... | collective-permute-start | bytes 862856 | tf_op jit(solution)/shard_map/ppermute | solution.py:51
  659.3 79.2 %collective-permute-start.132 = (bf16[642,224]{1,0:T(8,128)(2,1)}, bf16[642,224]{1,0:T(8,128)(2,1)}, u32[]{:S(2)}, u32[]{:S(2)}) collective-permute-start(bf16[642,224]{1,0:T(8,128)(2,1)} %pad_maximum_fusion.15), channel_id=1, source_target_pairs={{0,24},{8,16},{16,8},{24,0},{1,25},{9,17},{17,9},{25,1},{2,26},{10... | collective-permute-start | bytes 862856 | tf_op jit(solution)/shard_map/ppermute | solution.py:51
  707.2 43.2 %collective-permute-start.122 = (bf16[1,112,3584]{2,1,0:T(8,128)(2,1)}, bf16[1,112,3584]{2,1,0:T(8,128)(2,1)}, u32[]{:S(2)}, u32[]{:S(2)}) collective-permute-start(bf16[1,112,3584]{2,1,0:T(8,128)(2,1)} %constant_dynamic-slice_fusion.7), channel_id=1, source_target_pairs={{0,8},{8,0},{16,24},{24,16},{1,9},{9,1},{17,25},{25,17},{2,10},{10... | collective-permute-start | bytes 2408456 | tf_op jit(solution)/shard_map/ppermute | solution.py:51
  709.6 43.7 %collective-permute-start.126 = (bf16[1,112,3584]{2,1,0:T(8,128)(2,1)}, bf16[1,112,3584]{2,1,0:T(8,128)(2,1)}, u32[]{:S(2)}, u32[]{:S(2)}) collective-permute-start(bf16[1,112,3584]{2,1,0:T(8,128)(2,1)} %constant_dynamic-slice_fusion.6), channel_id=1, source_target_pairs={{0,16},{8,24},{16,0},{24,8},{1,17},{9,25},{17,1},{25,9},{2,18},{10... | collective-permute-start | bytes 2408456 | tf_op jit(solution)/shard_map/ppermute | solution.py:51
  738.4 37.3 %collective-permute-start.106 = (bf16[2,224,896]{2,1,0:T(8,128)(2,1)}, bf16[2,224,896]{2,1,0:T(8,128)(2,1)}, u32[]{:S(2)}, u32[]{:S(2)}) collective-permute-start(bf16[2,224,896]{2,1,0:T(8,128)(2,1)} %constant_dynamic-slice_fusion.2), channel_id=1, source_target_pairs={{0,8},{8,0},{16,24},{24,16},{1,9},{9,1},{17,25},{25,17},{2,10},{10... | collective-permute-start | bytes 2408456 | tf_op jit(solution)/shard_map/ppermute | solution.py:51
  760.6 32.9 %collective-permute-start.115 = (bf16[1,112,1792]{2,1,0:T(8,128)(2,1)S(1)}, bf16[1,112,1792]{2,1,0:T(8,128)(2,1)S(1)}, u32[]{:S(2)}, u32[]{:S(2)}) collective-permute-start(bf16[1,112,1792]{2,1,0:T(8,128)(2,1)S(1)} %dynamic-slice_convert_fusion.3), channel_id=1, source_target_pairs={{0,16},{8,24},{16,0},{24,8},{1,17},{9,25},{17,1},{25,9},{2,18},{10... | collective-permute-start | bytes 1204232 | tf_op jit(solution)/shard_map/ppermute | solution.py:51
  820.4 55.4 %collective-permute-start.117 = (bf16[1,112,3584]{2,1,0:T(8,128)(2,1)}, bf16[1,112,3584]{2,1,0:T(8,128)(2,1)}, u32[]{:S(2)}, u32[]{:S(2)}) collective-permute-start(bf16[1,112,3584]{2,1,0:T(8,128)(2,1)} %maximum_select_fusion.8), channel_id=1, source_target_pairs={{0,8},{8,0},{16,24},{24,16},{1,9},{9,1},{17,25},{25,17},{2,10},{10... | collective-permute-start | bytes 2408456 | tf_op jit(solution)/shard_map/ppermute | solution.py:51
  827.9 49.7 %collective-permute-start.121 = (bf16[1,112,3584]{2,1,0:T(8,128)(2,1)}, bf16[1,112,3584]{2,1,0:T(8,128)(2,1)}, u32[]{:S(2)}, u32[]{:S(2)}) collective-permute-start(bf16[1,112,3584]{2,1,0:T(8,128)(2,1)} %maximum_select_fusion.10), channel_id=1, source_target_pairs={{0,16},{8,24},{16,0},{24,8},{1,17},{9,25},{17,1},{25,9},{2,18},{10... | collective-permute-start | bytes 2408456 | tf_op jit(solution)/shard_map/ppermute | solution.py:51
  828.2 45.8 %collective-permute-start.109 = (bf16[2,224,896]{2,1,0:T(8,128)(2,1)S(1)}, bf16[2,224,896]{2,1,0:T(8,128)(2,1)}, u32[]{:S(2)}, u32[]{:S(2)}) collective-permute-start(bf16[2,224,896]{2,1,0:T(8,128)(2,1)S(1)} %maximum_select_fusion.6), channel_id=1, source_target_pairs={{0,8},{8,0},{16,24},{24,16},{1,9},{9,1},{17,25},{25,17},{2,10},{10... | collective-permute-start | bytes 2408456 | tf_op jit(solution)/shard_map/ppermute | solution.py:51
  844.5 36.8 %collective-permute-start.113 = (bf16[2,224,896]{2,1,0:T(8,128)(2,1)S(1)}, bf16[2,224,896]{2,1,0:T(8,128)(2,1)}, u32[]{:S(2)}, u32[]{:S(2)}) collective-permute-start(bf16[2,224,896]{2,1,0:T(8,128)(2,1)S(1)} %maximum_select_fusion.7), channel_id=1, source_target_pairs={{0,16},{8,24},{16,0},{24,8},{1,17},{9,25},{17,1},{25,9},{2,18},{10... | collective-permute-start | bytes 2408456 | tf_op jit(solution)/shard_map/ppermute | solution.py:51
  (239 other events, 2451.9 us)
